TPU v7x, 128 devices: a whole 4x4x4 slice. The times are simulated.
128 devices in a mesh: gx: 16 (over z, y_hi, core), gy: 8 (over y_lo, x).
Axes of the slice: x: 4, y: 4 (y_hi: 2, y_lo: 2; y = y_hi * 2 + y_lo), z: 4, core: 2. Of those that a mesh axis runs over, the one named last changes fastest.
Arguments:
- electric: float32 [3, 20, 128, 1024], P(None, None, 'gx', 'gy'), may hold values from -6 to 6
- magnetic: float32 [3, 20, 128, 1024], P(None, None, 'gx', 'gy'), may hold values from -6 to 6
- adjoint_electric: float32 [3, 20, 128, 1024], P(None, None, 'gx', 'gy'), may hold values from -6 to 6
- adjoint_magnetic: float32 [3, 20, 128, 1024], P(None, None, 'gx', 'gy'), may hold values from -6 to 6
- background: float32 [20, 128, 1024], P(None, 'gx', 'gy'), may hold values from 1 to 2.5
- absorb_x: int32 [128], P('gx'), may hold values from 0 to 12, as said below
- absorb_y: int32 [1024], P('gy'), may hold values from 0 to 12, as said below
- slab_offset: int32 [1], replicated, may hold values from 0 to 4
- design: float32 [16, 1024, 128], P(None, ('gx', 'gy')), may hold values from 0 to 1
- first_moment: float32 [16, 1024, 128], P(None, ('gx', 'gy')), may hold values from -1.2 to 1.2
- second_moment: float32 [16, 1024, 128], P(None, ('gx', 'gy')), may hold values from 0.01 to 1
Outputs:
- electric_final: float32 [3, 20, 128, 1024], P(None, None, 'gx', 'gy')
- magnetic_final: float32 [3, 20, 128, 1024], P(None, None, 'gx', 'gy')
- back_electric: float32 [3, 20, 128, 1024], P(None, None, 'gx', 'gy')
- back_magnetic: float32 [3, 20, 128, 1024], P(None, None, 'gx', 'gy')
- design_next: float32 [16, 1024, 128], P(None, ('gx', 'gy'))
- first_next: float32 [16, 1024, 128], P(None, ('gx', 'gy'))
- second_next: float32 [16, 1024, 128], P(None, ('gx', 'gy'))
Inputs may be any that keep to these rules, and one draw needn't show every extreme that they name: absorb_x[x] = max(0, 12 - x, x - (127 - d)) for one depth d of 6 to 12. absorb_y[y] = max(0, 12 - y, y - (1023 - d)) for one depth d of 6 to 12.
All inputs are finite; a program needn't handle non-finite values.
Results may differ from a plain program's by a relative error of at most 0.0001.
Values sent between devices are 32-bit elements; how exact they have to be, the bound alone decides.
No kernel may reach another device: no remote copies, remote signals or barrier semaphores. Data moves between devices by JAX's collectives and lax.ppermute only.
A program may use at most 128 MiB of HBM per device.

v0:
```python
import math

import jax
import jax.numpy as jnp
from jax import lax
from jax.experimental import pallas as pl
from jax.experimental.pallas import tpu as pltpu
from jax.sharding import PartitionSpec as P

NZ = 20
DZ = 16
STEPS = 4
RAD = 4
PML_DEPTH = 12

COURANT = 0.5
SIGMA_MAX = 0.4
CONTRAST = 3.0
SHARPNESS = 8.0
THRESHOLD = 0.5
LEARN_RATE = 0.02
BETA_ONE = 0.9
BETA_TWO = 0.999
BIAS_ONE = 1.0 - 0.9**10
BIAS_TWO = 1.0 - 0.999**10
ADAM_FLOOR = 1e-08

ROWS = 8
LANES = 128
SHARDS = 16
PLANES = 3 * NZ
FIELD_TILES = PLANES // 2
X_TILES = 4 * FIELD_TILES + NZ // 2 + 1
Y_TILES = 33


def gauss_taps(radius):
    spread = radius / 2.0
    raw_taps = [
        math.exp(-((position - radius) ** 2) / (2.0 * spread * spread))
        for position in range(2 * radius + 1)
    ]
    weight_sum = sum(raw_taps)
    return [weight_value / weight_sum for weight_value in raw_taps]


WEIGHTS = gauss_taps(RAD)


def roll(values, shift, axis):
    return pltpu.roll(values, shift % values.shape[axis], axis)


def filter_ring(values):
    total = WEIGHTS[RAD] * values
    for tap in range(1, RAD + 1):
        total = total + WEIGHTS[RAD + tap] * (roll(values, tap, 1) + roll(values, -tap, 1))
    return total


def filter_row(values, lane):
    total = WEIGHTS[RAD] * values
    for tap in range(1, RAD + 1):
        before = jnp.where(lane >= tap, roll(values, tap, 1), 0.0)
        after = jnp.where(lane < LANES - tap, roll(values, -tap, 1), 0.0)
        total = total + WEIGHTS[RAD + tap] * (before + after)
    return total


def iotas():
    shape = (ROWS, LANES)
    return lax.broadcasted_iota(jnp.int32, shape, 0), lax.broadcasted_iota(jnp.int32, shape, 1)


def pack_x_kernel(e, h, g, k, bg, absorb_x, absorb_y, xl, xr, dc):
    row, _ = iotas()
    low = row < 4

    def pair(first, second, index):
        xl[index] = jnp.where(low, first, roll(second, 4, 0))
        xr[index] = jnp.where(low, roll(first, 4, 0), second)

    def body(i, carry):
        for number, field in enumerate((e, h, g, k)):
            pair(field[2 * i], field[2 * i + 1], number * FIELD_TILES + i)
        return carry

    lax.fori_loop(0, FIELD_TILES, body, 0, unroll=5)
    for i in range(NZ // 2):
        pair(bg[2 * i], bg[2 * i + 1], 4 * FIELD_TILES + i)
    level_x = jnp.zeros((ROWS, LANES), jnp.float32)
    for i in range(ROWS):
        level_x = jnp.where(row == i, absorb_x[i].astype(jnp.float32), level_x)
    level_x = level_x / PML_DEPTH
    level_y = jnp.broadcast_to(absorb_y[...].astype(jnp.float32) / PML_DEPTH, (ROWS, LANES))
    damping = SIGMA_MAX * (level_x * level_x + level_y * level_y)
    decay = (1.0 - damping) / (1.0 + damping)
    coupling = COURANT / (1.0 + damping)
    dc[0] = decay
    dc[1] = coupling
    pair(decay, coupling, X_TILES - 1)


def pack_design_kernel(design, out):
    _, lane = iotas()
    group = lane // 16
    for kh in range(2):
        rows = [filter_row(design[8 * kh + kk], lane) for kk in range(8)]
        for a in range(SHARDS):
            total = roll(rows[0], 4 - 8 * a, 1)
            for kk in range(1, 8):
                total = jnp.where(group == kk, roll(rows[kk], 16 * kk + 4 - 8 * a, 1), total)
            out[a, kh] = total


def pack_y_kernel(e, h, g, k, bg, dc, rxl, rxr, yl, yr, hx):
    row, lane = iotas()
    low = row < 4
    group = lane // 8

    def halo(tile, odd):
        after, before = rxl[tile], rxr[tile]
        if odd:
            return jnp.where(low, roll(after, 4, 0), before)
        return jnp.where(low, after, roll(before, 4, 0))

    def put(totals, values, j):
        left = roll(values, 8 * j, 1)
        right = roll(values, 8 * j - 120, 1)
        if totals is None:
            return left, right
        return jnp.where(group == j, left, totals[0]), jnp.where(group == j, right, totals[1])

    for half, fields in enumerate(((e, h), (g, k))):

        def body(i, carry):
            totals = None
            for number, field in enumerate(fields):
                which = 2 * half + number
                for q in range(4):
                    edge = halo(which * FIELD_TILES + 2 * i + q // 2, q % 2)
                    hx[which * PLANES + 4 * i + q] = edge
                    totals = put(totals, field[4 * i + q], 8 * number + 2 * q)
                    totals = put(totals, edge, 8 * number + 2 * q + 1)
            yl[15 * half + i] = totals[0]
            yr[15 * half + i] = totals[1]
            return carry

        lax.fori_loop(0, 15, body, 0)
    for m in range(3):
        totals = None
        for q in range(8):
            p = 8 * m + q
            if p >= NZ + 2:
                continue
            edge = halo(4 * FIELD_TILES + p // 2, p % 2)
            hx[4 * PLANES + p] = edge
            totals = put(totals, bg[p] if p < NZ else dc[p - NZ], 2 * q)
            totals = put(totals, edge, 2 * q + 1)
        yl[30 + m] = totals[0]
        yr[30 + m] = totals[1]


def repack_design_kernel(ra, sb):
    b = lax.axis_index("gy")
    for dest in range(8):
        sb[dest, 0] = ra[2 * dest]
        sb[dest, 1] = ra[2 * dest + 1]
        before = ra[2 * dest - 1] if dest > 0 else jnp.zeros_like(ra[0])
        after = ra[2 * dest + 2] if dest < 7 else jnp.zeros_like(ra[0])
        sb[dest, 2] = jnp.where(b >= 4, before, after)


def main_kernel(
    offset_ref, e, h, g, k, bg, dc, hx, ryl, ryr, rb,
    eo, ho, go, ko, send,
    es, hs, gs, ks, gain, dcy, cpl, dx, ch, sn, sf, ft,
):
    offset = offset_ref[0]
    b = lax.axis_index("gy")
    _, lane = iotas()
    first_lanes = lane < 8
    last_lanes = lane >= 120
    top, bottom = pl.ds(0, 8), pl.ds(8, 8)
    near, far = pl.ds(0, 128), pl.ds(128, 128)

    def side(after, before, j):
        edge = jnp.where(last_lanes, roll(before, 120 - 8 * j, 1), 0.0)
        return jnp.where(first_lanes, roll(after, -8 * j, 1), edge)

    for half, pairs in enumerate((((e, es), (h, hs)), ((g, gs), (k, ks)))):
        for c in range(3):

            def unpack(i, carry):
                after, before = ryl[15 * half + 5 * c + i], ryr[15 * half + 5 * c + i]
                for number, (field, ext) in enumerate(pairs):
                    which = 2 * half + number
                    for q in range(4):
                        z = 4 * i + q
                        j = 8 * number + 2 * q
                        ext[c, z, top, near] = field[c * NZ + z]
                        ext[c, z, bottom, near] = hx[which * PLANES + c * NZ + z]
                        ext[c, z, top, far] = side(after, before, j)
                        ext[c, z, bottom, far] = side(after, before, j + 1)
                return carry

            lax.fori_loop(0, 5, unpack, 0)
    for p in range(NZ + 2):
        m, j = p // 8, 2 * (p % 8)
        own = bg[p] if p < NZ else dc[p - NZ]
        ext = gain.at[p] if p < NZ else (dcy, cpl)[p - NZ]
        ext[top, near] = own
        ext[bottom, near] = hx[4 * PLANES + p]
        ext[top, far] = side(ryl[30 + m], ryr[30 + m], j)
        ext[bottom, far] = side(ryl[30 + m], ryr[30 + m], j + 1)
    plane = jnp.zeros((16, 256), jnp.float32)
    for ext in (es, gs):
        for c in range(2):
            ext[c, NZ] = plane
    gain[NZ] = plane

    blank = jnp.zeros((96, LANES), jnp.float32)
    for kh in range(2):
        inner = jnp.concatenate([rb[j % 8, j // 8, kh] for j in range(16)], 0)
        outer = jnp.concatenate([rb[0, 2, kh], rb[1, 2, kh], blank, rb[6, 2, kh], rb[7, 2, kh]], 0)
        inner, outer = inner.T, outer.T
        for kk in range(8):
            rows = slice(16 * kk, 16 * kk + 16)
            both = jnp.concatenate([inner[rows], outer[rows]], 1)
            dx[8 * kh + kk] = roll(both, -4, 0)

    edge = math.tanh(SHARPNESS * THRESHOLD)

    def project(layer, carry):
        smooth = filter_ring(dx[layer])
        inner = jnp.tanh(SHARPNESS * (smooth - THRESHOLD))
        density = (edge + inner) / (2.0 * edge)
        slope = SHARPNESS * (1.0 - inner * inner) / (2.0 * edge)
        coupling = cpl[...]
        eps = gain[offset + layer] + CONTRAST * density
        eps = jnp.where(coupling == 0.0, 1.0, eps)
        gain[offset + layer] = eps
        factor = -CONTRAST * slope * ((coupling / eps) / eps)
        sf[layer] = factor[:8]
        return carry

    lax.fori_loop(0, DZ, project, 0)

    def invert(z, carry):
        coupling = cpl[...]
        eps = jnp.where(coupling == 0.0, 1.0, gain[z])
        gain[z] = coupling / eps
        sn[z] = jnp.zeros((8, 256), jnp.float32)
        return carry

    lax.fori_loop(0, NZ, invert, 0)

    def ahead(vx, vy, vz, vxn, vyn):
        cx = (roll(vz, -1, 1) - vz) - (vyn - vy)
        cy = (vxn - vx) - (roll(vz, -1, 0) - vz)
        cz = (roll(vy, -1, 0) - vy) - (roll(vx, -1, 1) - vx)
        return cx, cy, cz

    def behind(vx, vy, vz, vxp, vyp):
        cx = (vz - roll(vz, 1, 1)) - (vy - vyp)
        cy = (vx - vxp) - (vz - roll(vz, 1, 0))
        cz = (vy - roll(vy, 1, 0)) - (vx - roll(vx, 1, 1))
        return cx, cy, cz

    for step in range(STEPS):
        last = step == STEPS - 1

        def forward(z, carry):
            ex, ey, hxp, hyp = carry
            ez = es[2, z]
            exn, eyn = es[0, z + 1], es[1, z + 1]
            decay, coupling = dcy[...], cpl[...]
            curls = ahead(ex, ey, ez, exn, eyn)
            hn = [decay * hs[c, z] - coupling * curls[c] for c in range(3)]
            back = behind(hn[0], hn[1], hn[2], hxp, hyp)
            rate = gain[z]
            old = (ex, ey, ez)
            for c in range(3):
                ch[step, c, z] = back[c][:8]
                new = decay * old[c] + rate * back[c]
                if last:
                    eo[c * NZ + z] = new[:8, :128]
                    ho[c * NZ + z] = hn[c][:8, :128]
                else:
                    es[c, z] = new
                    hs[c, z] = hn[c]
            return exn, eyn, hn[0], hn[1]

        lax.fori_loop(0, NZ, forward, (es[0, 0], es[1, 0], plane, plane))

    for step in reversed(range(STEPS)):
        last = step == 0

        def backward(z, carry):
            wx, wy, mxp, myp = carry
            old = [gs[c, z] for c in range(3)]
            total = sn[z]
            for c in range(3):
                total = total + old[c][:8] * ch[step, c, z]
            sn[z] = total
            wz = gain[z] * old[2]
            following = gain[z + 1]
            wxn, wyn = following * gs[0, z + 1], following * gs[1, z + 1]
            decay, coupling = dcy[...], cpl[...]
            curls = ahead(wx, wy, wz, wxn, wyn)
            carried = [ks[c, z] + curls[c] for c in range(3)]
            mass = [coupling * carried[c] for c in range(3)]
            back = behind(mass[0], mass[1], mass[2], mxp, myp)
            for c in range(3):
                new = decay * old[c] - back[c]
                kept = decay * carried[c]
                if last:
                    go[c * NZ + z] = new[:8, :128]
                    ko[c * NZ + z] = kept[:8, :128]
                else:
                    gs[c, z] = new
                    ks[c, z] = kept
            return wxn, wyn, mass[0], mass[1]

        start = gain[0]
        lax.fori_loop(0, NZ, backward, (start * gs[0, 0], start * gs[1, 0], plane, plane))

    def sense(layer, carry):
        values = sn[offset + layer] * sf[layer]
        ft[pl.ds(pl.multiple_of(8 * layer, 8), 8), :] = filter_ring(values)[:, :128]
        return carry

    lax.fori_loop(0, DZ, sense, 0)

    def clear(i, carry):
        send[i] = jnp.zeros((ROWS, LANES), jnp.float32)
        return carry

    lax.fori_loop(0, 128, clear, 0, unroll=8)
    turned = ft[...].T
    for j in range(SHARDS):
        send[SHARDS * b + j] = turned[8 * j:8 * j + 8]


def adam_kernel(arrived, design, first, second, design_out, first_out, second_out):
    b = lax.axis_index("gx") // 2
    _, lane = iotas()
    group = lane // 8
    blocks = [arrived[8 * a + b] for a in range(SHARDS)]
    for layer in range(DZ):
        total = roll(blocks[0], -8 * layer, 1)
        for a in range(1, SHARDS):
            total = jnp.where(group == a, roll(blocks[a], 8 * a - 8 * layer, 1), total)
        gradient = filter_row(total, lane)
        first_next = BETA_ONE * first[layer] + (1.0 - BETA_ONE) * gradient
        second_next = BETA_TWO * second[layer] + (1.0 - BETA_TWO) * gradient * gradient
        update = LEARN_RATE * (first_next / BIAS_ONE)
        update = update / (jnp.sqrt(second_next / BIAS_TWO) + ADAM_FLOOR)
        design_out[layer] = jnp.clip(design[layer] - update, 0.0, 1.0)
        first_out[layer] = first_next
        second_out[layer] = second_next


def f32(*shape):
    return jax.ShapeDtypeStruct(shape, jnp.float32)


def call(kernel, outs, args, spaces, name, mebibytes, scratch=(), cost=1):
    out_specs = [pl.BlockSpec(memory_space=pltpu.VMEM) for _ in outs]
    return pl.pallas_call(
        kernel,
        out_shape=outs,
        in_specs=[pl.BlockSpec(memory_space=space) for space in spaces],
        out_specs=out_specs,
        scratch_shapes=list(scratch),
        compiler_params=pltpu.CompilerParams(vmem_limit_bytes=mebibytes << 20),
        cost_estimate=pl.CostEstimate(
            flops=cost * 1000000, bytes_accessed=cost * 1000000, transcendentals=0
        ),
        name=name,
    )(*args)


def shifted(block, axis, distance):
    count = lax.axis_size(axis)
    route = [(i, i + distance) for i in range(count) if 0 <= i + distance < count]
    return lax.ppermute(block, axis, route)


def local(
    electric,
    magnetic,
    adjoint_electric,
    adjoint_magnetic,
    background,
    absorb_x,
    absorb_y,
    slab_offset,
    design,
    first_moment,
    second_moment,
):
    vmem, smem = pltpu.VMEM, pltpu.SMEM
    fields = [
        field.reshape(PLANES, ROWS, LANES)
        for field in (electric, magnetic, adjoint_electric, adjoint_magnetic)
    ]
    xl, xr, dc = call(
        pack_x_kernel,
        [f32(X_TILES, ROWS, LANES), f32(X_TILES, ROWS, LANES), f32(2, ROWS, LANES)],
        (*fields, background, absorb_x, absorb_y.reshape(1, LANES)),
        [vmem] * 5 + [smem, vmem],
        "pack_x",
        8,
    )
    rxl = shifted(xl, "gx", -1)
    rxr = shifted(xr, "gx", 1)
    (sa,) = call(
        pack_design_kernel, [f32(SHARDS, 2, ROWS, LANES)], (design,), [vmem], "pack_design", 4
    )
    ra = lax.all_to_all(sa, "gx", split_axis=0, concat_axis=0, tiled=True)
    yl, yr, hx = call(
        pack_y_kernel,
        [
            f32(Y_TILES, ROWS, LANES),
            f32(Y_TILES, ROWS, LANES),
            f32(4 * PLANES + NZ + 2, ROWS, LANES),
        ],
        (*fields, background, dc, rxl, rxr),
        [vmem] * 8,
        "pack_y",
        8,
    )
    ryl = shifted(yl, "gy", -1)
    ryr = shifted(yr, "gy", 1)
    (sb,) = call(
        repack_design_kernel, [f32(8, 3, 2, ROWS, LANES)], (ra,), [vmem], "repack_design", 4
    )
    rb = lax.all_to_all(sb, "gy", split_axis=0, concat_axis=0, tiled=True)
    extended = vmem((3, NZ + 1, 16, 256), jnp.float32)
    eo, ho, go, ko, send = call(
        main_kernel,
        [f32(PLANES, ROWS, LANES)] * 4 + [f32(128, ROWS, LANES)],
        (slab_offset, *fields, background, dc, hx, ryl, ryr, rb),
        [smem] + [vmem] * 10,
        "time_steps",
        24,
        [
            extended,
            extended,
            extended,
            extended,
            vmem((NZ + 1, 16, 256), jnp.float32),
            vmem((16, 256), jnp.float32),
            vmem((16, 256), jnp.float32),
            vmem((DZ, 16, 256), jnp.float32),
            vmem((STEPS, 3, NZ, 8, 256), jnp.float32),
            vmem((NZ, 8, 256), jnp.float32),
            vmem((DZ, 8, 256), jnp.float32),
            vmem((128, 128), jnp.float32),
        ],
        10,
    )
    arrived = lax.all_to_all(send, ("gx", "gy"), split_axis=0, concat_axis=0, tiled=True)
    shard = f32(DZ, ROWS, LANES)
    design_next, first_next, second_next = call(
        adam_kernel,
        [shard] * 3,
        (arrived, design, first_moment, second_moment),
        [vmem] * 4,
        "adam",
        4,
    )
    shape = electric.shape
    return (
        eo.reshape(shape),
        ho.reshape(shape),
        go.reshape(shape),
        ko.reshape(shape),
        design_next,
        first_next,
        second_next,
    )


def solution(mesh):
    grid = P(None, None, "gx", "gy")
    rows = P(None, ("gx", "gy"), None)
    in_specs = (grid, grid, grid, grid, P(None, "gx", "gy"), P("gx"), P("gy"), P(), rows, rows, rows)
    out_specs = (grid, grid, grid, grid, rows, rows, rows)
    return jax.shard_map(local, mesh=mesh, in_specs=in_specs, out_specs=out_specs, check_vma=False)
```

profile of v0, /device:TPU:1, one launch (start us, length us, event | category | flops | bytes accessed | tf_op | source)
XLA Modules:
  0.0 109.4 jit_solution(8970456715832051385)
XLA Ops:
  0.6 0.0 copy-start
  0.6 0.9 copy-done
  1.6 0.0 copy-start.2
  1.6 0.9 copy-done.2
  2.5 0.0 copy-start.4
  2.5 0.9 copy-done.4
  3.5 0.0 copy-start.6
  3.5 0.9 copy-done.6
  4.4 0.0 copy-start.8
  4.4 0.9 copy-done.8
  5.3 0.0 copy-start.14
  5.3 0.7 copy-done.14
  6.0 0.0 copy-start.15
  6.0 0.7 copy-done.15
  6.6 0.0 copy-start.1
  6.6 0.0 copy-start.5
  6.6 0.0 copy-start.7
  6.6 0.0 copy-start.9
  6.6 1.5 %pack_x.1 = (f32[131,8,128]{2,1,0:T(8,128)}, f32[131,8,128]{2,1,0:T(8,128)S(1)}, f32[2,8,128]{2,1,0:T(8,128)S(1)}) custom-call(f32[60,8,128]{2,1,0:T(8,128)S(1)} %bitcast.9, f32[60,8,128]{2,1,0:T(8,128)S(1)} %bitcast.12, f32[60,8,128]{2,1,0:T(8,128)S(1)} %bitcast.15, f32[60,8,128]{2,1,0:T(8,128)S(1)} %bitcast.18, f32[20,8,128]{2,1,0:T(8,128)S(1)} %copy-done.8, ...), custom_call_target="tpu_custom_call" | custom-call | flops 1000000 | bytes 1000000 | tf_op jit(solution)/shard_map/pack_x/pallas_call | solution.py:370
  8.1 3.3 %collective-permute-start = (f32[131,8,128]{2,1,0:T(8,128)}, f32[131,8,128]{2,1,0:T(8,128)S(1)}, u32[]{:S(2)}, u32[]{:S(2)}) collective-permute-start(f32[131,8,128]{2,1,0:T(8,128)} %get-tuple-element.22), channel_id=1, source_target_pairs={{8,0},{16,8},{24,16},{32,24},{40,32},{48,40},{56,48},{64,56},{72,6... | collective-permute-start | bytes 1609736 | tf_op jit(solution)/shard_map/ppermute | solution.py:387
  11.4 4.8 %collective-permute-start.1 = (f32[131,8,128]{2,1,0:T(8,128)S(1)}, f32[131,8,128]{2,1,0:T(8,128)S(1)}, u32[]{:S(2)}, u32[]{:S(2)}) collective-permute-start(f32[131,8,128]{2,1,0:T(8,128)S(1)} %get-tuple-element.23), channel_id=1, source_target_pairs={{0,8},{8,16},{16,24},{24,32},{32,40},{40,48},{48,56},{56,64},{64,7... | collective-permute-start | bytes 1609736 | tf_op jit(solution)/shard_map/ppermute | solution.py:387
  16.2 0.0 copy-start.10
  16.2 0.8 copy-done.10
  17.1 0.6 pack_design.1
  17.7 16.0 %all_to_all.15.ra = f32[16,2,8,128]{3,2,1,0:T(8,128)S(1)} all-to-all(f32[16,2,8,128]{3,2,1,0:T(8,128)S(1)} %pack_design.1), channel_id=1, replica_groups=mesh['gx'=16,'gy'=8] {'gx'}, dimensions={0} | all-to-all | bytes 262144 | tf_op jit(solution)/shard_map/all_to_all | solution.py:421
  33.6 0.7 repack_design.1
  34.3 4.1 %all-to-all-start.1 = ((f32[8,3,2,8,128]{4,3,2,1,0:T(8,128)}), f32[8,3,2,8,128]{4,3,2,1,0:T(8,128)S(1)}, u32[]{:S(2)}, u32[]{:S(2)}) async-start(f32[8,3,2,8,128]{4,3,2,1,0:T(8,128)} %repack_design.1), calls=%async_computation.1 | async-start | bytes 393216 | tf_op jit(solution)/shard_map/all_to_all | solution.py:439
  38.5 0.0 collective-permute-done.rxl
  38.5 0.0 collective-permute-done.1.rxr
  38.5 0.0 copy-done.1
  38.5 0.0 copy-done.3
  38.5 0.0 copy-done.5
  38.5 0.0 copy-done.7
  38.5 0.0 copy-done.9
  38.5 3.9 %pack_y.1 = (f32[33,8,128]{2,1,0:T(8,128)}, f32[33,8,128]{2,1,0:T(8,128)S(1)}, f32[262,8,128]{2,1,0:T(8,128)S(1)}) custom-call(f32[60,8,128]{2,1,0:T(8,128)S(1)} %bitcast.10, f32[60,8,128]{2,1,0:T(8,128)S(1)} %bitcast.13, f32[60,8,128]{2,1,0:T(8,128)S(1)} %bitcast.16, f32[60,8,128]{2,1,0:T(8,128)S(1)} %bitcast.19, f32[20,8,128]{2,1,0:T(8,128)S(1)} %copy-done.9, ...), custom_call_target="tpu_custom_call" | custom-call | flops 1000000 | bytes 1000000 | tf_op jit(solution)/shard_map/pack_y/pallas_call | solution.py:370
  42.4 1.3 %collective-permute-start.2 = (f32[33,8,128]{2,1,0:T(8,128)}, f32[33,8,128]{2,1,0:T(8,128)S(1)}, u32[]{:S(2)}, u32[]{:S(2)}) collective-permute-start(f32[33,8,128]{2,1,0:T(8,128)} %get-tuple-element.25), channel_id=1, source_target_pairs={{1,0},{2,1},{3,2},{4,3},{5,4},{6,5},{7,6},{9,8},{10,9},{11,10},{12... | collective-permute-start | bytes 405512 | tf_op jit(solution)/shard_map/ppermute | solution.py:387
  43.7 4.0 %collective-permute-start.3 = (f32[33,8,128]{2,1,0:T(8,128)S(1)}, f32[33,8,128]{2,1,0:T(8,128)S(1)}, u32[]{:S(2)}, u32[]{:S(2)}) collective-permute-start(f32[33,8,128]{2,1,0:T(8,128)S(1)} %get-tuple-element.26), channel_id=1, source_target_pairs={{0,1},{1,2},{2,3},{3,4},{4,5},{5,6},{6,7},{8,9},{9,10},{10,11},{11... | collective-permute-start | bytes 405512 | tf_op jit(solution)/shard_map/ppermute | solution.py:387
  48.3 0.0 all-to-all-done.1.rb
  48.3 0.4 collective-permute-done.2.ryl
  48.7 1.0 collective-permute-done.3.ryr
  49.6 32.9 %time_steps.1 = (f32[60,8,128]{2,1,0:T(8,128)}, f32[60,8,128]{2,1,0:T(8,128)}, f32[60,8,128]{2,1,0:T(8,128)}, f32[60,8,128]{2,1,0:T(8,128)}, f32[128,8,128]{2,1,0:T(8,128)S(1)}) custom-call(s32[1]{0:T(128)S(6)} %copy.18.offset_ref, f32[60,8,128]{2,1,0:T(8,128)S(1)} %bitcast.11, f32[60,8,128]{2,1,0:T(8,128)S(1)} %bitcast.14, f32[60,8,128]{2,1,0:T(8,128)S(1)} %bitcast.17, ...), custom_call_target="tpu_custom_call" | custom-call | flops 10000000 | bytes 10000000 | tf_op jit(solution)/shard_map/time_steps/pallas_call | solution.py:370
  82.5 0.0 copy-start.11
  82.5 0.0 copy-start.12
  82.5 25.2 %all_to_all.16.arrived = f32[128,8,128]{2,1,0:T(8,128)S(1)} all-to-all(f32[128,8,128]{2,1,0:T(8,128)S(1)} %get-tuple-element.31), channel_id=1, replica_groups=mesh['gx'=16,'gy'=8] {'gx','gy'}, dimensions={0} | all-to-all | bytes 1048576 | tf_op jit(solution)/shard_map/all_to_all | solution.py:464
  107.7 0.0 copy-done.11
  107.7 0.0 copy-done.12
  107.7 0.0 copy-done.13
  107.7 1.7 %adam.1 = (f32[16,8,128]{2,1,0:T(8,128)}, f32[16,8,128]{2,1,0:T(8,128)}, f32[16,8,128]{2,1,0:T(8,128)}) custom-call(f32[128,8,128]{2,1,0:T(8,128)S(1)} %all_to_all.16.arrived, f32[16,8,128]{2,1,0:T(8,128)S(1)} %copy-done.11, f32[16,8,128]{2,1,0:T(8,128)S(1)} %copy-done.12, f32[16,8,128]{2,1,0:T(8,128)S(1)} %copy-done.13), custom_call_target="tpu_custom_call" | custom-call | flops 1000000 | bytes 1000000 | tf_op jit(solution)/shard_map/adam/pallas_call | solution.py:370
  (2 shorter events, 0.0 us)
Async XLA Ops:
  0.6 0.9 copy-start
  1.6 0.9 copy-start.2
  2.5 0.9 copy-start.4
  3.5 0.9 copy-start.6
  4.4 0.9 copy-start.8
  5.3 0.7 copy-start.14
  6.0 0.7 copy-start.15
  6.6 31.9 %copy-start.1 = (f32[3,20,8,128]{3,2,1,0:T(8,128)S(1)}, f32[3,20,8,128]{3,2,1,0:T(8,128)}, u32[]{:S(2)}) copy-start(f32[3,20,8,128]{3,2,1,0:T(8,128)} %param.11) | copy-start | bytes 737284
  6.6 31.9 %copy-start.3 = (f32[3,20,8,128]{3,2,1,0:T(8,128)S(1)}, f32[3,20,8,128]{3,2,1,0:T(8,128)}, u32[]{:S(2)}) copy-start(f32[3,20,8,128]{3,2,1,0:T(8,128)} %param.12) | copy-start | bytes 737284
  6.6 31.9 %copy-start.5 = (f32[3,20,8,128]{3,2,1,0:T(8,128)S(1)}, f32[3,20,8,128]{3,2,1,0:T(8,128)}, u32[]{:S(2)}) copy-start(f32[3,20,8,128]{3,2,1,0:T(8,128)} %param.13) | copy-start | bytes 737284
  6.6 31.9 %copy-start.7 = (f32[3,20,8,128]{3,2,1,0:T(8,128)S(1)}, f32[3,20,8,128]{3,2,1,0:T(8,128)}, u32[]{:S(2)}) copy-start(f32[3,20,8,128]{3,2,1,0:T(8,128)} %param.14) | copy-start | bytes 737284
  6.6 31.9 %copy-start.9 = (f32[20,8,128]{2,1,0:T(8,128)S(1)}, f32[20,8,128]{2,1,0:T(8,128)}, u32[]{:S(2)}) copy-start(f32[20,8,128]{2,1,0:T(8,128)} %bg.5) | copy-start | bytes 245764
  8.1 30.4 %collective-permute-start = (f32[131,8,128]{2,1,0:T(8,128)}, f32[131,8,128]{2,1,0:T(8,128)S(1)}, u32[]{:S(2)}, u32[]{:S(2)}) collective-permute-start(f32[131,8,128]{2,1,0:T(8,128)} %get-tuple-element.22), channel_id=1, source_target_pairs={{8,0},{16,8},{24,16},{32,24},{40,32},{48,40},{56,48},{64,56},{72,6... | collective-permute-start | bytes 1609736 | tf_op jit(solution)/shard_map/ppermute | solution.py:387
  11.4 27.1 %collective-permute-start.1 = (f32[131,8,128]{2,1,0:T(8,128)S(1)}, f32[131,8,128]{2,1,0:T(8,128)S(1)}, u32[]{:S(2)}, u32[]{:S(2)}) collective-permute-start(f32[131,8,128]{2,1,0:T(8,128)S(1)} %get-tuple-element.23), channel_id=1, source_target_pairs={{0,8},{8,16},{16,24},{24,32},{32,40},{40,48},{48,56},{56,64},{64,7... | collective-permute-start | bytes 1609736 | tf_op jit(solution)/shard_map/ppermute | solution.py:387
  16.2 0.8 copy-start.10
  34.3 14.0 %all-to-all-start.1 = ((f32[8,3,2,8,128]{4,3,2,1,0:T(8,128)}), f32[8,3,2,8,128]{4,3,2,1,0:T(8,128)S(1)}, u32[]{:S(2)}, u32[]{:S(2)}) async-start(f32[8,3,2,8,128]{4,3,2,1,0:T(8,128)} %repack_design.1), calls=%async_computation.1 | async-start | bytes 393216 | tf_op jit(solution)/shard_map/all_to_all | solution.py:439
  42.4 6.3 %collective-permute-start.2 = (f32[33,8,128]{2,1,0:T(8,128)}, f32[33,8,128]{2,1,0:T(8,128)S(1)}, u32[]{:S(2)}, u32[]{:S(2)}) collective-permute-start(f32[33,8,128]{2,1,0:T(8,128)} %get-tuple-element.25), channel_id=1, source_target_pairs={{1,0},{2,1},{3,2},{4,3},{5,4},{6,5},{7,6},{9,8},{10,9},{11,10},{12... | collective-permute-start | bytes 405512 | tf_op jit(solution)/shard_map/ppermute | solution.py:387
  43.7 6.0 %collective-permute-start.3 = (f32[33,8,128]{2,1,0:T(8,128)S(1)}, f32[33,8,128]{2,1,0:T(8,128)S(1)}, u32[]{:S(2)}, u32[]{:S(2)}) collective-permute-start(f32[33,8,128]{2,1,0:T(8,128)S(1)} %get-tuple-element.26), channel_id=1, source_target_pairs={{0,1},{1,2},{2,3},{3,4},{4,5},{5,6},{6,7},{8,9},{9,10},{10,11},{11... | collective-permute-start | bytes 405512 | tf_op jit(solution)/shard_map/ppermute | solution.py:387
  82.5 25.2 %copy-start.11 = (f32[16,8,128]{2,1,0:T(8,128)S(1)}, f32[16,8,128]{2,1,0:T(8,128)}, u32[]{:S(2)}) copy-start(f32[16,8,128]{2,1,0:T(8,128)} %design.3) | copy-start | bytes 196612
  82.5 25.2 %copy-start.12 = (f32[16,8,128]{2,1,0:T(8,128)S(1)}, f32[16,8,128]{2,1,0:T(8,128)}, u32[]{:S(2)}) copy-start(f32[16,8,128]{2,1,0:T(8,128)} %first.1) | copy-start | bytes 196612
  82.5 25.2 %copy-start.13 = (f32[16,8,128]{2,1,0:T(8,128)S(1)}, f32[16,8,128]{2,1,0:T(8,128)}, u32[]{:S(2)}) copy-start(f32[16,8,128]{2,1,0:T(8,128)} %second.1) | copy-start | bytes 196612
where the time goes:
time: 110 us; the launch traced here: 109 us
  Pallas kernels  41.2 us (37%)
  blocking collectives  41.1 us (37%)
  starting transfers between devices  17.5 us (16%)
  local copies, waits for them, and re-layouts  6.83 us (6%)
  between operations  1.43 us (1%)
  waiting for transfers between devices  1.31 us (1%)
    pallas_call x6, Pallas kernels, call(): pl.pallas_call(kernel, out_shape=outs, in_specs=[pl.BlockSpec(memory_spac...  41.2 us
    all_to_all x1, blocking collectives, local(): lax.all_to_all(send, ('gx', 'gy'), split_axis=0, concat_axis=0, tiled=True)  25.2 us
    all_to_all x1, blocking collectives, local(): ra = lax.all_to_all(sa, 'gx', split_axis=0, concat_axis=0, tiled=True)  16 us
    ppermute x4, starting transfers between devices, shifted(): return lax.ppermute(block, axis, route)  13.4 us
    unnamed x32, local copies, waits for them, and re-layouts  6.83 us
    all_to_all x1, starting transfers between devices, local(): rb = lax.all_to_all(sb, 'gy', split_axis=0, concat_axis=0, tiled=True)  4.13 us
  transfers between devices with their start and end apart: 5, of which 2 were waited for; matrix products, arithmetic and copies ran while one was open for 0% of the time, Pallas kernels for 5%

commit v1 on v0

--- a/solution.py
+++ b/solution.py
@@ -125,28 +125,30 @@
         return jnp.where(low, after, roll(before, 4, 0))
 
     def put(totals, values, j):
-        left = roll(values, 8 * j, 1)
-        right = roll(values, 8 * j - 120, 1)
+        moved = roll(values, 8 * j, 1)
         if totals is None:
-            return left, right
-        return jnp.where(group == j, left, totals[0]), jnp.where(group == j, right, totals[1])
+            return moved, moved
+        before = (j - 1) % 16
+        return jnp.where(group == j, moved, totals[0]), jnp.where(group == before, moved, totals[1])
 
     for half, fields in enumerate(((e, h), (g, k))):
 
-        def body(i, carry):
-            totals = None
-            for number, field in enumerate(fields):
-                which = 2 * half + number
-                for q in range(4):
-                    edge = halo(which * FIELD_TILES + 2 * i + q // 2, q % 2)
-                    hx[which * PLANES + 4 * i + q] = edge
-                    totals = put(totals, field[4 * i + q], 8 * number + 2 * q)
-                    totals = put(totals, edge, 8 * number + 2 * q + 1)
-            yl[15 * half + i] = totals[0]
-            yr[15 * half + i] = totals[1]
+        def body(c, carry):
+            for n in range(5):
+                i = 5 * c + n
+                totals = None
+                for number, field in enumerate(fields):
+                    which = 2 * half + number
+                    for q in range(4):
+                        edge = halo(which * FIELD_TILES + 2 * i + q // 2, q % 2)
+                        hx[which * PLANES + 4 * i + q] = edge
+                        totals = put(totals, field[4 * i + q], 8 * number + 2 * q)
+                        totals = put(totals, edge, 8 * number + 2 * q + 1)
+                yl[15 * half + i] = totals[0]
+                yr[15 * half + i] = totals[1]
             return carry
 
-        lax.fori_loop(0, 15, body, 0)
+        lax.fori_loop(0, 3, body, 0)
     for m in range(3):
         totals = None
         for q in range(8):
@@ -174,25 +176,27 @@
 def main_kernel(
     offset_ref, e, h, g, k, bg, dc, hx, ryl, ryr, rb,
     eo, ho, go, ko, send,
-    es, hs, gs, ks, gain, dcy, cpl, dx, ch, sn, sf, ft,
+    es, hs, gs, ks, gain, dcy, cpl, dx, ch, sn, sf, rot, ws, band, sems,
 ):
     offset = offset_ref[0]
     b = lax.axis_index("gy")
     _, lane = iotas()
-    first_lanes = lane < 8
-    last_lanes = lane >= 120
+    group = lane // 8
+    even = group % 2 == 0
+    edges = (group == 0) | (group == 15)
     top, bottom = pl.ds(0, 8), pl.ds(8, 8)
     near, far = pl.ds(0, 128), pl.ds(128, 128)
 
-    def side(after, before, j):
-        edge = jnp.where(last_lanes, roll(before, 120 - 8 * j, 1), 0.0)
-        return jnp.where(first_lanes, roll(after, -8 * j, 1), edge)
+    def sides(m):
+        after, before = ryl[m], ryr[m]
+        mixed = jnp.where(even, after, before), jnp.where(even, before, after)
+        return lambda j: jnp.where(edges, roll(mixed[j % 2], -8 * j, 1), 0.0)
 
     for half, pairs in enumerate((((e, es), (h, hs)), ((g, gs), (k, ks)))):
-        for c in range(3):
-
-            def unpack(i, carry):
-                after, before = ryl[15 * half + 5 * c + i], ryr[15 * half + 5 * c + i]
+
+        def unpack(c, carry):
+            for i in range(5):
+                side = sides(15 * half + 5 * c + i)
                 for number, (field, ext) in enumerate(pairs):
                     which = 2 * half + number
                     for q in range(4):
@@ -200,40 +204,53 @@
                         j = 8 * number + 2 * q
                         ext[c, z, top, near] = field[c * NZ + z]
                         ext[c, z, bottom, near] = hx[which * PLANES + c * NZ + z]
-                        ext[c, z, top, far] = side(after, before, j)
-                        ext[c, z, bottom, far] = side(after, before, j + 1)
-                return carry
-
-            lax.fori_loop(0, 5, unpack, 0)
-    for p in range(NZ + 2):
-        m, j = p // 8, 2 * (p % 8)
-        own = bg[p] if p < NZ else dc[p - NZ]
-        ext = gain.at[p] if p < NZ else (dcy, cpl)[p - NZ]
-        ext[top, near] = own
-        ext[bottom, near] = hx[4 * PLANES + p]
-        ext[top, far] = side(ryl[30 + m], ryr[30 + m], j)
-        ext[bottom, far] = side(ryl[30 + m], ryr[30 + m], j + 1)
+                        ext[c, z, top, far] = side(j)
+                        ext[c, z, bottom, far] = side(j + 1)
+            return carry
+
+        lax.fori_loop(0, 3, unpack, 0)
+    for m in range(3):
+        side = sides(30 + m)
+        for q in range(8):
+            p = 8 * m + q
+            if p >= NZ + 2:
+                continue
+            own = bg[p] if p < NZ else dc[p - NZ]
+            ext = gain.at[p] if p < NZ else (dcy, cpl)[p - NZ]
+            ext[top, near] = own
+            ext[bottom, near] = hx[4 * PLANES + p]
+            ext[top, far] = side(2 * q)
+            ext[bottom, far] = side(2 * q + 1)
     plane = jnp.zeros((16, 256), jnp.float32)
-    for ext in (es, gs):
-        for c in range(2):
-            ext[c, NZ] = plane
-    gain[NZ] = plane
-
+
+    shape = (256, 256)
+    apart = lax.broadcasted_iota(jnp.int32, shape, 0) - lax.broadcasted_iota(jnp.int32, shape, 1)
+    apart = (apart + RAD) & 255
+    taps = jnp.zeros(shape, jnp.float32)
+    for tap in range(2 * RAD + 1):
+        taps = jnp.where(apart == tap, WEIGHTS[tap], taps)
+    band[...] = taps
     blank = jnp.zeros((96, LANES), jnp.float32)
     for kh in range(2):
-        inner = jnp.concatenate([rb[j % 8, j // 8, kh] for j in range(16)], 0)
-        outer = jnp.concatenate([rb[0, 2, kh], rb[1, 2, kh], blank, rb[6, 2, kh], rb[7, 2, kh]], 0)
-        inner, outer = inner.T, outer.T
+        arrived = jnp.concatenate(
+            [rb[j % 8, j // 8, kh] for j in range(16)]
+            + [rb[0, 2, kh], rb[1, 2, kh], blank, rb[6, 2, kh], rb[7, 2, kh]],
+            0,
+        )
+        smooth = lax.dot_general(
+            arrived,
+            band[...],
+            (((0,), (0,)), ((), ())),
+            precision=lax.Precision.HIGHEST,
+            preferred_element_type=jnp.float32,
+        )
         for kk in range(8):
-            rows = slice(16 * kk, 16 * kk + 16)
-            both = jnp.concatenate([inner[rows], outer[rows]], 1)
-            dx[8 * kh + kk] = roll(both, -4, 0)
+            dx[8 * kh + kk] = roll(smooth[16 * kk:16 * kk + 16], -4, 0)
 
     edge = math.tanh(SHARPNESS * THRESHOLD)
 
     def project(layer, carry):
-        smooth = filter_ring(dx[layer])
-        inner = jnp.tanh(SHARPNESS * (smooth - THRESHOLD))
+        inner = jnp.tanh(SHARPNESS * (dx[layer] - THRESHOLD))
         density = (edge + inner) / (2.0 * edge)
         slope = SHARPNESS * (1.0 - inner * inner) / (2.0 * edge)
         coupling = cpl[...]
@@ -244,7 +261,7 @@
         sf[layer] = factor[:8]
         return carry
 
-    lax.fori_loop(0, DZ, project, 0)
+    lax.fori_loop(0, DZ, project, 0, unroll=4)
 
     def invert(z, carry):
         coupling = cpl[...]
@@ -253,93 +270,109 @@
         sn[z] = jnp.zeros((8, 256), jnp.float32)
         return carry
 
-    lax.fori_loop(0, NZ, invert, 0)
-
-    def ahead(vx, vy, vz, vxn, vyn):
-        cx = (roll(vz, -1, 1) - vz) - (vyn - vy)
-        cy = (vxn - vx) - (roll(vz, -1, 0) - vz)
-        cz = (roll(vy, -1, 0) - vy) - (roll(vx, -1, 1) - vx)
+    lax.fori_loop(0, NZ, invert, 0, unroll=4)
+
+    def ahead(v, vn, ry, rx):
+        cx = (ry - v[2]) - (vn[1] - v[1])
+        cy = (vn[0] - v[0]) - (roll(v[2], -1, 0) - v[2])
+        cz = (roll(v[1], -1, 0) - v[1]) - (rx - v[0])
         return cx, cy, cz
 
-    def behind(vx, vy, vz, vxp, vyp):
-        cx = (vz - roll(vz, 1, 1)) - (vy - vyp)
-        cy = (vx - vxp) - (vz - roll(vz, 1, 0))
-        cz = (vy - roll(vy, 1, 0)) - (vx - roll(vx, 1, 1))
+    def behind(v, vp, ry, rx):
+        cx = (v[2] - ry) - (v[1] - vp[1])
+        cy = (v[0] - vp[0]) - (v[2] - roll(v[2], 1, 0))
+        cz = (v[1] - roll(v[1], 1, 0)) - (v[0] - rx)
         return cx, cy, cz
 
-    for step in range(STEPS):
-        last = step == STEPS - 1
-
-        def forward(z, carry):
-            ex, ey, hxp, hyp = carry
-            ez = es[2, z]
-            exn, eyn = es[0, z + 1], es[1, z + 1]
-            decay, coupling = dcy[...], cpl[...]
-            curls = ahead(ex, ey, ez, exn, eyn)
-            hn = [decay * hs[c, z] - coupling * curls[c] for c in range(3)]
-            back = behind(hn[0], hn[1], hn[2], hxp, hyp)
+    def turn(field, shift):
+        for z in range(NZ):
+            rot[0, z] = roll(field[2, z], shift, 1)
+            rot[1, z] = roll(field[0, z], shift, 1)
+
+    def forward(step, carry):
+        decay, coupling = dcy[...], cpl[...]
+        turn(es, -1)
+        for z in range(NZ):
+            now = [es[c, z] for c in range(3)]
+            later = [es[c, z + 1] if z + 1 < NZ else plane for c in range(2)]
+            curls = ahead(now, later, rot[0, z], rot[1, z])
+            for c in range(3):
+                hs[c, z] = decay * hs[c, z] - coupling * curls[c]
+        turn(hs, 1)
+        for z in range(NZ):
+            now = [hs[c, z] for c in range(3)]
+            former = [hs[c, z - 1] if z > 0 else plane for c in range(2)]
+            back = behind(now, former, rot[0, z], rot[1, z])
             rate = gain[z]
-            old = (ex, ey, ez)
             for c in range(3):
                 ch[step, c, z] = back[c][:8]
-                new = decay * old[c] + rate * back[c]
-                if last:
-                    eo[c * NZ + z] = new[:8, :128]
-                    ho[c * NZ + z] = hn[c][:8, :128]
-                else:
-                    es[c, z] = new
-                    hs[c, z] = hn[c]
-            return exn, eyn, hn[0], hn[1]
-
-        lax.fori_loop(0, NZ, forward, (es[0, 0], es[1, 0], plane, plane))
-
-    for step in reversed(range(STEPS)):
-        last = step == 0
-
-        def backward(z, carry):
-            wx, wy, mxp, myp = carry
-            old = [gs[c, z] for c in range(3)]
+                es[c, z] = decay * es[c, z] + rate * back[c]
+        return carry
+
+    lax.fori_loop(0, STEPS, forward, 0)
+    copies = []
+
+    def export(ext, out, number):
+        for c in range(3):
+            copy = pltpu.make_async_copy(
+                ext.at[c, :, top, near], out.at[pl.ds(c * NZ, NZ)], sems.at[3 * number + c]
+            )
+            copy.start()
+            copies.append(copy)
+
+    export(es, eo, 0)
+    export(hs, ho, 1)
+
+    def backward(number, carry):
+        step = STEPS - 1 - number
+        decay, coupling = dcy[...], cpl[...]
+        for z in range(NZ):
+            rate = gain[z]
             total = sn[z]
             for c in range(3):
-                total = total + old[c][:8] * ch[step, c, z]
+                now = gs[c, z]
+                total = total + now[:8] * ch[step, c, z]
+                ws[c, z] = rate * now
             sn[z] = total
-            wz = gain[z] * old[2]
-            following = gain[z + 1]
-            wxn, wyn = following * gs[0, z + 1], following * gs[1, z + 1]
-            decay, coupling = dcy[...], cpl[...]
-            curls = ahead(wx, wy, wz, wxn, wyn)
-            carried = [ks[c, z] + curls[c] for c in range(3)]
-            mass = [coupling * carried[c] for c in range(3)]
-            back = behind(mass[0], mass[1], mass[2], mxp, myp)
+        turn(ws, -1)
+        for z in range(NZ):
+            now = [ws[c, z] for c in range(3)]
+            later = [ws[c, z + 1] if z + 1 < NZ else plane for c in range(2)]
+            curls = ahead(now, later, rot[0, z], rot[1, z])
             for c in range(3):
-                new = decay * old[c] - back[c]
-                kept = decay * carried[c]
-                if last:
-                    go[c * NZ + z] = new[:8, :128]
-                    ko[c * NZ + z] = kept[:8, :128]
-                else:
-                    gs[c, z] = new
-                    ks[c, z] = kept
-            return wxn, wyn, mass[0], mass[1]
-
-        start = gain[0]
-        lax.fori_loop(0, NZ, backward, (start * gs[0, 0], start * gs[1, 0], plane, plane))
-
-    def sense(layer, carry):
-        values = sn[offset + layer] * sf[layer]
-        ft[pl.ds(pl.multiple_of(8 * layer, 8), 8), :] = filter_ring(values)[:, :128]
+                carried = ks[c, z] + curls[c]
+                ks[c, z] = decay * carried
+                ws[c, z] = coupling * carried
+        turn(ws, 1)
+        for z in range(NZ):
+            now = [ws[c, z] for c in range(3)]
+            former = [ws[c, z - 1] if z > 0 else plane for c in range(2)]
+            back = behind(now, former, rot[0, z], rot[1, z])
+            for c in range(3):
+                gs[c, z] = decay * gs[c, z] - back[c]
         return carry
 
-    lax.fori_loop(0, DZ, sense, 0)
+    lax.fori_loop(0, STEPS, backward, 0)
+    export(gs, go, 2)
+    export(ks, ko, 3)
 
     def clear(i, carry):
         send[i] = jnp.zeros((ROWS, LANES), jnp.float32)
         return carry
 
-    lax.fori_loop(0, 128, clear, 0, unroll=8)
-    turned = ft[...].T
+    lax.fori_loop(0, 128, clear, 0, unroll=16)
+    values = jnp.concatenate([sn[offset + layer] * sf[layer] for layer in range(DZ)], 0)
+    turned = lax.dot_general(
+        band[:, :128],
+        values,
+        (((0,), (1,)), ((), ())),
+        precision=lax.Precision.HIGHEST,
+        preferred_element_type=jnp.float32,
+    )
     for j in range(SHARDS):
         send[SHARDS * b + j] = turned[8 * j:8 * j + 8]
+    for copy in copies:
+        copy.wait()
 
 
 def adam_kernel(arrived, design, first, second, design_out, first_out, second_out):
@@ -365,8 +398,10 @@
     return jax.ShapeDtypeStruct(shape, jnp.float32)
 
 
-def call(kernel, outs, args, spaces, name, mebibytes, scratch=(), cost=1):
-    out_specs = [pl.BlockSpec(memory_space=pltpu.VMEM) for _ in outs]
+def call(kernel, outs, args, spaces, name, mebibytes, scratch=(), cost=1, away=0):
+    out_specs = [
+        pl.BlockSpec(memory_space=pl.ANY if i < away else pltpu.VMEM) for i in range(len(outs))
+    ]
     return pl.pallas_call(
         kernel,
         out_shape=outs,
@@ -437,7 +472,7 @@
         repack_design_kernel, [f32(8, 3, 2, ROWS, LANES)], (ra,), [vmem], "repack_design", 4
     )
     rb = lax.all_to_all(sb, "gy", split_axis=0, concat_axis=0, tiled=True)
-    extended = vmem((3, NZ + 1, 16, 256), jnp.float32)
+    extended = vmem((3, NZ, 16, 256), jnp.float32)
     eo, ho, go, ko, send = call(
         main_kernel,
         [f32(PLANES, ROWS, LANES)] * 4 + [f32(128, ROWS, LANES)],
@@ -450,16 +485,20 @@
             extended,
             extended,
             extended,
-            vmem((NZ + 1, 16, 256), jnp.float32),
+            vmem((NZ, 16, 256), jnp.float32),
             vmem((16, 256), jnp.float32),
             vmem((16, 256), jnp.float32),
             vmem((DZ, 16, 256), jnp.float32),
             vmem((STEPS, 3, NZ, 8, 256), jnp.float32),
             vmem((NZ, 8, 256), jnp.float32),
             vmem((DZ, 8, 256), jnp.float32),
-            vmem((128, 128), jnp.float32),
+            vmem((2, NZ, 16, 256), jnp.float32),
+            vmem((3, NZ, 16, 256), jnp.float32),
+            vmem((256, 256), jnp.float32),
+            pltpu.SemaphoreType.DMA((12,)),
         ],
         10,
+        4,
     )
     arrived = lax.all_to_all(send, ("gx", "gy"), split_axis=0, concat_axis=0, tiled=True)
     shard = f32(DZ, ROWS, LANES)

time: 110 us -> 82.8 us (0.75)
  Pallas kernels: 41.2 us -> 13.9 us
    pallas_call x6, Pallas kernels: 41.2 us -> 13.9 us  [call(): pl.pallas_call(kernel, out_shape=outs, in_specs=[pl.BlockSpec(memory_spac...]
  transfers between devices with their start and end apart: 5 -> 5, of which waited for: 2 -> 2; matrix products, arithmetic and copies ran while one was open for 0% -> 0% of each run, Pallas kernels for 5% -> 4%
where the time goes in v1:
time: 82.8 us; the launch traced here: 82.2 us
  blocking collectives  41.2 us (50%)
  starting transfers between devices  17.5 us (21%)
  Pallas kernels  13.9 us (17%)
  local copies, waits for them, and re-layouts  6.84 us (8%)
  between operations  1.46 us (2%)
  waiting for transfers between devices  1.31 us (2%)
    all_to_all x1, blocking collectives, local(): lax.all_to_all(send, ('gx', 'gy'), split_axis=0, concat_axis=0, tiled=True)  25.2 us
    all_to_all x1, blocking collectives, local(): ra = lax.all_to_all(sa, 'gx', split_axis=0, concat_axis=0, tiled=True)  16 us
    pallas_call x6, Pallas kernels, call(): pl.pallas_call(kernel, out_shape=outs, in_specs=[pl.BlockSpec(memory_spac...  13.9 us
    ppermute x4, starting transfers between devices, shifted(): return lax.ppermute(block, axis, route)  13.4 us
    unnamed x32, local copies, waits for them, and re-layouts  6.84 us
    all_to_all x1, starting transfers between devices, local(): rb = lax.all_to_all(sb, 'gy', split_axis=0, concat_axis=0, tiled=True)  4.13 us
  transfers between devices with their start and end apart: 5, of which 2 were waited for; matrix products, arithmetic and copies ran while one was open for 0% of the time, Pallas kernels for 4%

profile of v1, /device:TPU:1, one launch (start us, length us, event | category | flops | bytes accessed | tf_op | source)
XLA Modules:
  0.0 82.2 jit_solution(7638858336595749931)
XLA Ops:
  0.6 0.0 copy-start
  0.6 0.9 %copy-done = f32[3,20,8,128]{3,2,1,0:T(8,128)S(1)} copy-done((f32[3,20,8,128]{3,2,1,0:T(8,128)S(1)}, f32[3,20,8,128]{3,2,1,0:T(8,128)}, u32[]{:S(2)}) %copy-start) | copy-done | bytes 245784
  1.6 0.0 copy-start.2
  1.6 0.9 %copy-done.2 = f32[3,20,8,128]{3,2,1,0:T(8,128)S(1)} copy-done((f32[3,20,8,128]{3,2,1,0:T(8,128)S(1)}, f32[3,20,8,128]{3,2,1,0:T(8,128)}, u32[]{:S(2)}) %copy-start.2) | copy-done | bytes 245784
  2.5 0.0 copy-start.4
  2.5 0.9 %copy-done.4 = f32[3,20,8,128]{3,2,1,0:T(8,128)S(1)} copy-done((f32[3,20,8,128]{3,2,1,0:T(8,128)S(1)}, f32[3,20,8,128]{3,2,1,0:T(8,128)}, u32[]{:S(2)}) %copy-start.4) | copy-done | bytes 245784
  3.5 0.0 copy-start.6
  3.5 0.9 %copy-done.6 = f32[3,20,8,128]{3,2,1,0:T(8,128)S(1)} copy-done((f32[3,20,8,128]{3,2,1,0:T(8,128)S(1)}, f32[3,20,8,128]{3,2,1,0:T(8,128)}, u32[]{:S(2)}) %copy-start.6) | copy-done | bytes 245784
  4.4 0.0 copy-start.8
  4.4 0.9 %copy-done.8 = f32[20,8,128]{2,1,0:T(8,128)S(1)} copy-done((f32[20,8,128]{2,1,0:T(8,128)S(1)}, f32[20,8,128]{2,1,0:T(8,128)}, u32[]{:S(2)}) %copy-start.8) | copy-done | bytes 81944
  5.3 0.0 copy-start.14
  5.3 0.7 copy-done.14
  6.0 0.0 copy-start.15
  6.0 0.7 copy-done.15
  6.6 0.0 copy-start.1
  6.6 0.0 copy-start.5
  6.6 0.0 copy-start.9
  6.6 1.5 %pack_x.1 = (f32[131,8,128]{2,1,0:T(8,128)}, f32[131,8,128]{2,1,0:T(8,128)S(1)}, f32[2,8,128]{2,1,0:T(8,128)S(1)}) custom-call(f32[60,8,128]{2,1,0:T(8,128)S(1)} %bitcast.9, f32[60,8,128]{2,1,0:T(8,128)S(1)} %bitcast.12, f32[60,8,128]{2,1,0:T(8,128)S(1)} %bitcast.15, f32[60,8,128]{2,1,0:T(8,128)S(1)} %bitcast.18, f32[20,8,128]{2,1,0:T(8,128)S(1)} %copy-done.8, ...), custom_call_target="tpu_custom_call" | custom-call | flops 1000000 | bytes 1000000 | tf_op jit(solution)/shard_map/pack_x/pallas_call | solution.py:405
  8.1 3.3 %collective-permute-start = (f32[131,8,128]{2,1,0:T(8,128)}, f32[131,8,128]{2,1,0:T(8,128)S(1)}, u32[]{:S(2)}, u32[]{:S(2)}) collective-permute-start(f32[131,8,128]{2,1,0:T(8,128)} %get-tuple-element.22), channel_id=1, source_target_pairs={{8,0},{16,8},{24,16},{32,24},{40,32},{48,40},{56,48},{64,56},{72,6... | collective-permute-start | bytes 1609736 | tf_op jit(solution)/shard_map/ppermute | solution.py:422
  11.4 4.8 %collective-permute-start.1 = (f32[131,8,128]{2,1,0:T(8,128)S(1)}, f32[131,8,128]{2,1,0:T(8,128)S(1)}, u32[]{:S(2)}, u32[]{:S(2)}) collective-permute-start(f32[131,8,128]{2,1,0:T(8,128)S(1)} %get-tuple-element.23), channel_id=1, source_target_pairs={{0,8},{8,16},{16,24},{24,32},{32,40},{40,48},{48,56},{56,64},{64,7... | collective-permute-start | bytes 1609736 | tf_op jit(solution)/shard_map/ppermute | solution.py:422
  16.2 0.0 copy-start.10
  16.2 0.8 %copy-done.10 = f32[16,8,128]{2,1,0:T(8,128)S(1)} copy-done((f32[16,8,128]{2,1,0:T(8,128)S(1)}, f32[16,8,128]{2,1,0:T(8,128)}, u32[]{:S(2)}) %copy-start.10) | copy-done | bytes 65560
  17.1 0.6 pack_design.1
  17.7 16.0 %all_to_all.15.ra = f32[16,2,8,128]{3,2,1,0:T(8,128)S(1)} all-to-all(f32[16,2,8,128]{3,2,1,0:T(8,128)S(1)} %pack_design.1), channel_id=1, replica_groups=mesh['gx'=16,'gy'=8] {'gx'}, dimensions={0} | all-to-all | bytes 262144 | tf_op jit(solution)/shard_map/all_to_all | solution.py:456
  33.6 0.7 repack_design.1
  34.3 4.1 %all-to-all-start.1 = ((f32[8,3,2,8,128]{4,3,2,1,0:T(8,128)}), f32[8,3,2,8,128]{4,3,2,1,0:T(8,128)S(1)}, u32[]{:S(2)}, u32[]{:S(2)}) async-start(f32[8,3,2,8,128]{4,3,2,1,0:T(8,128)} %repack_design.1), calls=%async_computation.1 | async-start | bytes 393216 | tf_op jit(solution)/shard_map/all_to_all | solution.py:474
  38.5 0.0 collective-permute-done.rxl
  38.5 0.0 collective-permute-done.1.rxr
  38.5 0.0 copy-done.1
  38.5 0.0 copy-done.3
  38.5 0.0 copy-done.5
  38.5 0.0 copy-done.7
  38.5 0.0 copy-done.9
  38.5 1.7 %pack_y.1 = (f32[33,8,128]{2,1,0:T(8,128)}, f32[33,8,128]{2,1,0:T(8,128)S(1)}, f32[262,8,128]{2,1,0:T(8,128)S(1)}) custom-call(f32[60,8,128]{2,1,0:T(8,128)S(1)} %bitcast.10, f32[60,8,128]{2,1,0:T(8,128)S(1)} %bitcast.13, f32[60,8,128]{2,1,0:T(8,128)S(1)} %bitcast.16, f32[60,8,128]{2,1,0:T(8,128)S(1)} %bitcast.19, f32[20,8,128]{2,1,0:T(8,128)S(1)} %copy-done.9, ...), custom_call_target="tpu_custom_call" | custom-call | flops 1000000 | bytes 1000000 | tf_op jit(solution)/shard_map/pack_y/pallas_call | solution.py:405
  40.2 1.3 %collective-permute-start.2 = (f32[33,8,128]{2,1,0:T(8,128)}, f32[33,8,128]{2,1,0:T(8,128)S(1)}, u32[]{:S(2)}, u32[]{:S(2)}) collective-permute-start(f32[33,8,128]{2,1,0:T(8,128)} %get-tuple-element.25), channel_id=1, source_target_pairs={{1,0},{2,1},{3,2},{4,3},{5,4},{6,5},{7,6},{9,8},{10,9},{11,10},{12... | collective-permute-start | bytes 405512 | tf_op jit(solution)/shard_map/ppermute | solution.py:422
  41.5 4.0 %collective-permute-start.3 = (f32[33,8,128]{2,1,0:T(8,128)S(1)}, f32[33,8,128]{2,1,0:T(8,128)S(1)}, u32[]{:S(2)}, u32[]{:S(2)}) collective-permute-start(f32[33,8,128]{2,1,0:T(8,128)S(1)} %get-tuple-element.26), channel_id=1, source_target_pairs={{0,1},{1,2},{2,3},{3,4},{4,5},{5,6},{6,7},{8,9},{9,10},{10,11},{11... | collective-permute-start | bytes 405512 | tf_op jit(solution)/shard_map/ppermute | solution.py:422
  46.2 0.0 all-to-all-done.1.rb
  46.2 0.4 collective-permute-done.2.ryl
  46.5 1.0 %collective-permute-done.3.ryr = f32[33,8,128]{2,1,0:T(8,128)S(1)} collective-permute-done((f32[33,8,128]{2,1,0:T(8,128)S(1)}, f32[33,8,128]{2,1,0:T(8,128)S(1)}, u32[]{:S(2)}, u32[]{:S(2)}) %collective-permute-start.3) | collective-permute-done | bytes 135200 | tf_op jit(solution)/shard_map/ppermute | solution.py:422
  47.5 7.7 %time_steps.1 = (f32[60,8,128]{2,1,0:T(8,128)}, f32[60,8,128]{2,1,0:T(8,128)}, f32[60,8,128]{2,1,0:T(8,128)}, f32[60,8,128]{2,1,0:T(8,128)}, f32[128,8,128]{2,1,0:T(8,128)S(1)}) custom-call(s32[1]{0:T(128)S(6)} %copy.18.offset_ref, f32[60,8,128]{2,1,0:T(8,128)S(1)} %bitcast.11, f32[60,8,128]{2,1,0:T(8,128)S(1)} %bitcast.14, f32[60,8,128]{2,1,0:T(8,128)S(1)} %bitcast.17, ...), custom_call_target="tpu_custom_call" | custom-call | flops 10000000 | bytes 10000000 | tf_op jit(solution)/shard_map/time_steps/pallas_call | solution.py:405
  55.2 0.0 copy-start.11
  55.2 0.0 copy-start.12
  55.2 0.0 copy-start.13
  55.3 25.2 %all_to_all.16.arrived = f32[128,8,128]{2,1,0:T(8,128)S(1)} all-to-all(f32[128,8,128]{2,1,0:T(8,128)S(1)} %get-tuple-element.31), channel_id=1, replica_groups=mesh['gx'=16,'gy'=8] {'gx','gy'}, dimensions={0} | all-to-all | bytes 1048576 | tf_op jit(solution)/shard_map/all_to_all | solution.py:503
  80.4 0.0 copy-done.11
  80.4 0.0 copy-done.12
  80.4 0.0 copy-done.13
  80.4 1.7 %adam.1 = (f32[16,8,128]{2,1,0:T(8,128)}, f32[16,8,128]{2,1,0:T(8,128)}, f32[16,8,128]{2,1,0:T(8,128)}) custom-call(f32[128,8,128]{2,1,0:T(8,128)S(1)} %all_to_all.16.arrived, f32[16,8,128]{2,1,0:T(8,128)S(1)} %copy-done.11, f32[16,8,128]{2,1,0:T(8,128)S(1)} %copy-done.12, f32[16,8,128]{2,1,0:T(8,128)S(1)} %copy-done.13), custom_call_target="tpu_custom_call" | custom-call | flops 1000000 | bytes 1000000 | tf_op jit(solution)/shard_map/adam/pallas_call | solution.py:405
  (2 shorter events, 0.0 us)
Async XLA Ops:
  0.6 0.9 %copy-start = (f32[3,20,8,128]{3,2,1,0:T(8,128)S(1)}, f32[3,20,8,128]{3,2,1,0:T(8,128)}, u32[]{:S(2)}) copy-start(f32[3,20,8,128]{3,2,1,0:T(8,128)} %param.11) | copy-start | bytes 737284
  1.6 0.9 %copy-start.2 = (f32[3,20,8,128]{3,2,1,0:T(8,128)S(1)}, f32[3,20,8,128]{3,2,1,0:T(8,128)}, u32[]{:S(2)}) copy-start(f32[3,20,8,128]{3,2,1,0:T(8,128)} %param.12) | copy-start | bytes 737284
  2.5 0.9 %copy-start.4 = (f32[3,20,8,128]{3,2,1,0:T(8,128)S(1)}, f32[3,20,8,128]{3,2,1,0:T(8,128)}, u32[]{:S(2)}) copy-start(f32[3,20,8,128]{3,2,1,0:T(8,128)} %param.13) | copy-start | bytes 737284
  3.5 0.9 %copy-start.6 = (f32[3,20,8,128]{3,2,1,0:T(8,128)S(1)}, f32[3,20,8,128]{3,2,1,0:T(8,128)}, u32[]{:S(2)}) copy-start(f32[3,20,8,128]{3,2,1,0:T(8,128)} %param.14) | copy-start | bytes 737284
  4.4 0.9 %copy-start.8 = (f32[20,8,128]{2,1,0:T(8,128)S(1)}, f32[20,8,128]{2,1,0:T(8,128)}, u32[]{:S(2)}) copy-start(f32[20,8,128]{2,1,0:T(8,128)} %bg.5) | copy-start | bytes 245764
  5.3 0.7 copy-start.14
  6.0 0.7 copy-start.15
  6.6 31.9 %copy-start.1 = (f32[3,20,8,128]{3,2,1,0:T(8,128)S(1)}, f32[3,20,8,128]{3,2,1,0:T(8,128)}, u32[]{:S(2)}) copy-start(f32[3,20,8,128]{3,2,1,0:T(8,128)} %param.11) | copy-start | bytes 737284
  6.6 31.9 %copy-start.3 = (f32[3,20,8,128]{3,2,1,0:T(8,128)S(1)}, f32[3,20,8,128]{3,2,1,0:T(8,128)}, u32[]{:S(2)}) copy-start(f32[3,20,8,128]{3,2,1,0:T(8,128)} %param.12) | copy-start | bytes 737284
  6.6 31.9 %copy-start.5 = (f32[3,20,8,128]{3,2,1,0:T(8,128)S(1)}, f32[3,20,8,128]{3,2,1,0:T(8,128)}, u32[]{:S(2)}) copy-start(f32[3,20,8,128]{3,2,1,0:T(8,128)} %param.13) | copy-start | bytes 737284
  6.6 31.9 %copy-start.7 = (f32[3,20,8,128]{3,2,1,0:T(8,128)S(1)}, f32[3,20,8,128]{3,2,1,0:T(8,128)}, u32[]{:S(2)}) copy-start(f32[3,20,8,128]{3,2,1,0:T(8,128)} %param.14) | copy-start | bytes 737284
  6.6 31.9 %copy-start.9 = (f32[20,8,128]{2,1,0:T(8,128)S(1)}, f32[20,8,128]{2,1,0:T(8,128)}, u32[]{:S(2)}) copy-start(f32[20,8,128]{2,1,0:T(8,128)} %bg.5) | copy-start | bytes 245764
  8.1 30.4 %collective-permute-start = (f32[131,8,128]{2,1,0:T(8,128)}, f32[131,8,128]{2,1,0:T(8,128)S(1)}, u32[]{:S(2)}, u32[]{:S(2)}) collective-permute-start(f32[131,8,128]{2,1,0:T(8,128)} %get-tuple-element.22), channel_id=1, source_target_pairs={{8,0},{16,8},{24,16},{32,24},{40,32},{48,40},{56,48},{64,56},{72,6... | collective-permute-start | bytes 1609736 | tf_op jit(solution)/shard_map/ppermute | solution.py:422
  11.4 27.1 %collective-permute-start.1 = (f32[131,8,128]{2,1,0:T(8,128)S(1)}, f32[131,8,128]{2,1,0:T(8,128)S(1)}, u32[]{:S(2)}, u32[]{:S(2)}) collective-permute-start(f32[131,8,128]{2,1,0:T(8,128)S(1)} %get-tuple-element.23), channel_id=1, source_target_pairs={{0,8},{8,16},{16,24},{24,32},{32,40},{40,48},{48,56},{56,64},{64,7... | collective-permute-start | bytes 1609736 | tf_op jit(solution)/shard_map/ppermute | solution.py:422
  16.2 0.8 %copy-start.10 = (f32[16,8,128]{2,1,0:T(8,128)S(1)}, f32[16,8,128]{2,1,0:T(8,128)}, u32[]{:S(2)}) copy-start(f32[16,8,128]{2,1,0:T(8,128)} %design.3) | copy-start | bytes 196612
  34.3 11.8 %all-to-all-start.1 = ((f32[8,3,2,8,128]{4,3,2,1,0:T(8,128)}), f32[8,3,2,8,128]{4,3,2,1,0:T(8,128)S(1)}, u32[]{:S(2)}, u32[]{:S(2)}) async-start(f32[8,3,2,8,128]{4,3,2,1,0:T(8,128)} %repack_design.1), calls=%async_computation.1 | async-start | bytes 393216 | tf_op jit(solution)/shard_map/all_to_all | solution.py:474
  40.2 6.3 %collective-permute-start.2 = (f32[33,8,128]{2,1,0:T(8,128)}, f32[33,8,128]{2,1,0:T(8,128)S(1)}, u32[]{:S(2)}, u32[]{:S(2)}) collective-permute-start(f32[33,8,128]{2,1,0:T(8,128)} %get-tuple-element.25), channel_id=1, source_target_pairs={{1,0},{2,1},{3,2},{4,3},{5,4},{6,5},{7,6},{9,8},{10,9},{11,10},{12... | collective-permute-start | bytes 405512 | tf_op jit(solution)/shard_map/ppermute | solution.py:422
  41.5 6.0 %collective-permute-start.3 = (f32[33,8,128]{2,1,0:T(8,128)S(1)}, f32[33,8,128]{2,1,0:T(8,128)S(1)}, u32[]{:S(2)}, u32[]{:S(2)}) collective-permute-start(f32[33,8,128]{2,1,0:T(8,128)S(1)} %get-tuple-element.26), channel_id=1, source_target_pairs={{0,1},{1,2},{2,3},{3,4},{4,5},{5,6},{6,7},{8,9},{9,10},{10,11},{11... | collective-permute-start | bytes 405512 | tf_op jit(solution)/shard_map/ppermute | solution.py:422
  55.2 25.2 %copy-start.11 = (f32[16,8,128]{2,1,0:T(8,128)S(1)}, f32[16,8,128]{2,1,0:T(8,128)}, u32[]{:S(2)}) copy-start(f32[16,8,128]{2,1,0:T(8,128)} %design.3) | copy-start | bytes 196612
  55.2 25.2 %copy-start.12 = (f32[16,8,128]{2,1,0:T(8,128)S(1)}, f32[16,8,128]{2,1,0:T(8,128)}, u32[]{:S(2)}) copy-start(f32[16,8,128]{2,1,0:T(8,128)} %first.1) | copy-start | bytes 196612
  55.2 25.2 %copy-start.13 = (f32[16,8,128]{2,1,0:T(8,128)S(1)}, f32[16,8,128]{2,1,0:T(8,128)}, u32[]{:S(2)}) copy-start(f32[16,8,128]{2,1,0:T(8,128)} %second.1) | copy-start | bytes 196612

commit v2 on v1

--- a/solution.py
+++ b/solution.py
@@ -6,6 +6,7 @@
 from jax.experimental import pallas as pl
 from jax.experimental.pallas import tpu as pltpu
 from jax.sharding import PartitionSpec as P
+
 
 NZ = 20
 DZ = 16
@@ -51,13 +52,6 @@
     return pltpu.roll(values, shift % values.shape[axis], axis)
 
 
-def filter_ring(values):
-    total = WEIGHTS[RAD] * values
-    for tap in range(1, RAD + 1):
-        total = total + WEIGHTS[RAD + tap] * (roll(values, tap, 1) + roll(values, -tap, 1))
-    return total
-
-
 def filter_row(values, lane):
     total = WEIGHTS[RAD] * values
     for tap in range(1, RAD + 1):
@@ -72,57 +66,82 @@
     return lax.broadcasted_iota(jnp.int32, shape, 0), lax.broadcasted_iota(jnp.int32, shape, 1)
 
 
-def pack_x_kernel(e, h, g, k, bg, absorb_x, absorb_y, xl, xr, dc):
-    row, _ = iotas()
+def pack_kernel(
+    e, h, g, k, bg, absorb_x, absorb_y, design,
+    out, x1, x2, planes,
+    rows_ref, level_x_ref, level_y_ref, sems,
+):
+    loads = [
+        pltpu.make_async_copy(design, rows_ref, sems.at[0]),
+        pltpu.make_async_copy(absorb_x, level_x_ref, sems.at[1]),
+        pltpu.make_async_copy(absorb_y, level_y_ref, sems.at[2]),
+    ]
+    for number, field in enumerate((e, h, g, k, bg)):
+        count = field.shape[0]
+        target = planes.at[pl.ds(number * PLANES, count)]
+        loads.append(pltpu.make_async_copy(field, target, sems.at[3 + number]))
+    for load in loads:
+        load.start()
+    row, lane = iotas()
     low = row < 4
 
-    def pair(first, second, index):
-        xl[index] = jnp.where(low, first, roll(second, 4, 0))
-        xr[index] = jnp.where(low, roll(first, 4, 0), second)
-
-    def body(i, carry):
-        for number, field in enumerate((e, h, g, k)):
-            pair(field[2 * i], field[2 * i + 1], number * FIELD_TILES + i)
-        return carry
-
-    lax.fori_loop(0, FIELD_TILES, body, 0, unroll=5)
-    for i in range(NZ // 2):
-        pair(bg[2 * i], bg[2 * i + 1], 4 * FIELD_TILES + i)
-    level_x = jnp.zeros((ROWS, LANES), jnp.float32)
-    for i in range(ROWS):
-        level_x = jnp.where(row == i, absorb_x[i].astype(jnp.float32), level_x)
-    level_x = level_x / PML_DEPTH
-    level_y = jnp.broadcast_to(absorb_y[...].astype(jnp.float32) / PML_DEPTH, (ROWS, LANES))
-    damping = SIGMA_MAX * (level_x * level_x + level_y * level_y)
-    decay = (1.0 - damping) / (1.0 + damping)
-    coupling = COURANT / (1.0 + damping)
-    dc[0] = decay
-    dc[1] = coupling
-    pair(decay, coupling, X_TILES - 1)
-
-
-def pack_design_kernel(design, out):
-    _, lane = iotas()
     group = lane // 16
+    loads[0].wait()
     for kh in range(2):
-        rows = [filter_row(design[8 * kh + kk], lane) for kk in range(8)]
+        rows = [filter_row(rows_ref[8 * kh + kk], lane) for kk in range(8)]
         for a in range(SHARDS):
             total = roll(rows[0], 4 - 8 * a, 1)
             for kk in range(1, 8):
                 total = jnp.where(group == kk, roll(rows[kk], 16 * kk + 4 - 8 * a, 1), total)
             out[a, kh] = total
 
-
-def pack_y_kernel(e, h, g, k, bg, dc, rxl, rxr, yl, yr, hx):
+    loads[1].wait()
+    loads[2].wait()
+    level_x = jnp.zeros((ROWS, LANES), jnp.float32)
+    for i in range(ROWS):
+        level_x = jnp.where(row == i, level_x_ref[i].astype(jnp.float32), level_x)
+    level_x = level_x / PML_DEPTH
+    level_y = jnp.broadcast_to(level_y_ref[...].astype(jnp.float32) / PML_DEPTH, (ROWS, LANES))
+    damping = SIGMA_MAX * (level_x * level_x + level_y * level_y)
+    planes[4 * PLANES + NZ] = (1.0 - damping) / (1.0 + damping)
+    planes[4 * PLANES + NZ + 1] = COURANT / (1.0 + damping)
+
+    turned = lax.axis_index("gx") % 2 == 1
+
+    def pair(index):
+        first, second = planes[2 * index], planes[2 * index + 1]
+        before = jnp.where(low, first, roll(second, 4, 0))
+        after = jnp.where(low, roll(first, 4, 0), second)
+        x1[index] = jnp.where(turned, before, after)
+        x2[index] = jnp.where(turned, after, before)
+
+    for number in range(4):
+        loads[3 + number].wait()
+        for i in range(FIELD_TILES):
+            pair(number * FIELD_TILES + i)
+    loads[7].wait()
+    for i in range(NZ // 2 + 1):
+        pair(4 * FIELD_TILES + i)
+
+
+def pack_y_kernel(planes, rx1, rx2, y1, y2, hx):
     row, lane = iotas()
     low = row < 4
     group = lane // 8
 
+    turned_x = lax.axis_index("gx") % 2 == 1
+    turned_y = lax.axis_index("gy") % 2 == 1
+
     def halo(tile, odd):
-        after, before = rxl[tile], rxr[tile]
+        after = jnp.where(turned_x, rx2[tile], rx1[tile])
+        before = jnp.where(turned_x, rx1[tile], rx2[tile])
         if odd:
             return jnp.where(low, roll(after, 4, 0), before)
         return jnp.where(low, after, roll(before, 4, 0))
+
+    def send(index, before, after):
+        y1[index] = jnp.where(turned_y, before, after)
+        y2[index] = jnp.where(turned_y, after, before)
 
     def put(totals, values, j):
         moved = roll(values, 8 * j, 1)
@@ -131,21 +150,20 @@
         before = (j - 1) % 16
         return jnp.where(group == j, moved, totals[0]), jnp.where(group == before, moved, totals[1])
 
-    for half, fields in enumerate(((e, h), (g, k))):
+    for half in range(2):
 
         def body(c, carry):
             for n in range(5):
                 i = 5 * c + n
                 totals = None
-                for number, field in enumerate(fields):
+                for number in range(2):
                     which = 2 * half + number
                     for q in range(4):
                         edge = halo(which * FIELD_TILES + 2 * i + q // 2, q % 2)
                         hx[which * PLANES + 4 * i + q] = edge
-                        totals = put(totals, field[4 * i + q], 8 * number + 2 * q)
+                        totals = put(totals, planes[which * PLANES + 4 * i + q], 8 * number + 2 * q)
                         totals = put(totals, edge, 8 * number + 2 * q + 1)
-                yl[15 * half + i] = totals[0]
-                yr[15 * half + i] = totals[1]
+                send(15 * half + i, *totals)
             return carry
 
         lax.fori_loop(0, 3, body, 0)
@@ -157,10 +175,9 @@
                 continue
             edge = halo(4 * FIELD_TILES + p // 2, p % 2)
             hx[4 * PLANES + p] = edge
-            totals = put(totals, bg[p] if p < NZ else dc[p - NZ], 2 * q)
+            totals = put(totals, planes[4 * PLANES + p], 2 * q)
             totals = put(totals, edge, 2 * q + 1)
-        yl[30 + m] = totals[0]
-        yr[30 + m] = totals[1]
+        send(30 + m, *totals)
 
 
 def repack_design_kernel(ra, sb):
@@ -174,11 +191,10 @@
 
 
 def main_kernel(
-    offset_ref, e, h, g, k, bg, dc, hx, ryl, ryr, rb,
+    offset_ref, planes, hx, ry1, ry2, rb,
     eo, ho, go, ko, send,
     es, hs, gs, ks, gain, dcy, cpl, dx, ch, sn, sf, rot, ws, band, sems,
 ):
-    offset = offset_ref[0]
     b = lax.axis_index("gy")
     _, lane = iotas()
     group = lane // 8
@@ -187,22 +203,25 @@
     top, bottom = pl.ds(0, 8), pl.ds(8, 8)
     near, far = pl.ds(0, 128), pl.ds(128, 128)
 
+    turned_y = b % 2 == 1
+
     def sides(m):
-        after, before = ryl[m], ryr[m]
+        after = jnp.where(turned_y, ry2[m], ry1[m])
+        before = jnp.where(turned_y, ry1[m], ry2[m])
         mixed = jnp.where(even, after, before), jnp.where(even, before, after)
         return lambda j: jnp.where(edges, roll(mixed[j % 2], -8 * j, 1), 0.0)
 
-    for half, pairs in enumerate((((e, es), (h, hs)), ((g, gs), (k, ks)))):
+    for half, pairs in enumerate(((es, hs), (gs, ks))):
 
         def unpack(c, carry):
             for i in range(5):
                 side = sides(15 * half + 5 * c + i)
-                for number, (field, ext) in enumerate(pairs):
+                for number, ext in enumerate(pairs):
                     which = 2 * half + number
                     for q in range(4):
                         z = 4 * i + q
                         j = 8 * number + 2 * q
-                        ext[c, z, top, near] = field[c * NZ + z]
+                        ext[c, z, top, near] = planes[which * PLANES + c * NZ + z]
                         ext[c, z, bottom, near] = hx[which * PLANES + c * NZ + z]
                         ext[c, z, top, far] = side(j)
                         ext[c, z, bottom, far] = side(j + 1)
@@ -215,9 +234,8 @@
             p = 8 * m + q
             if p >= NZ + 2:
                 continue
-            own = bg[p] if p < NZ else dc[p - NZ]
             ext = gain.at[p] if p < NZ else (dcy, cpl)[p - NZ]
-            ext[top, near] = own
+            ext[top, near] = planes[4 * PLANES + p]
             ext[bottom, near] = hx[4 * PLANES + p]
             ext[top, far] = side(2 * q)
             ext[bottom, far] = side(2 * q + 1)
@@ -248,6 +266,7 @@
             dx[8 * kh + kk] = roll(smooth[16 * kk:16 * kk + 16], -4, 0)
 
     edge = math.tanh(SHARPNESS * THRESHOLD)
+    offset = offset_ref[0]
 
     def project(layer, carry):
         inner = jnp.tanh(SHARPNESS * (dx[layer] - THRESHOLD))
@@ -398,28 +417,39 @@
     return jax.ShapeDtypeStruct(shape, jnp.float32)
 
 
-def call(kernel, outs, args, spaces, name, mebibytes, scratch=(), cost=1, away=0):
-    out_specs = [
-        pl.BlockSpec(memory_space=pl.ANY if i < away else pltpu.VMEM) for i in range(len(outs))
-    ]
+def near_by(*shape):
+    return pltpu.VMEM(shape, jnp.float32)
+
+
+def call(kernel, outs, args, mebibytes, scratch=(), cost=1, far_args=(), scalar_args=(), far_outs=()):
+    def spec(far):
+        return pl.BlockSpec(memory_space=pltpu.HBM if far else pltpu.VMEM)
+
     return pl.pallas_call(
         kernel,
         out_shape=outs,
-        in_specs=[pl.BlockSpec(memory_space=space) for space in spaces],
-        out_specs=out_specs,
+        in_specs=[
+            pl.BlockSpec(memory_space=pltpu.SMEM) if i in scalar_args else spec(i in far_args)
+            for i in range(len(args))
+        ],
+        out_specs=[spec(i in far_outs) for i in range(len(outs))],
         scratch_shapes=list(scratch),
         compiler_params=pltpu.CompilerParams(vmem_limit_bytes=mebibytes << 20),
         cost_estimate=pl.CostEstimate(
             flops=cost * 1000000, bytes_accessed=cost * 1000000, transcendentals=0
         ),
-        name=name,
-    )(*args)
-
-
-def shifted(block, axis, distance):
+    )(
+        *[
+            pltpu.with_memory_space_constraint(arg, pltpu.HBM) if i in far_args else arg
+            for i, arg in enumerate(args)
+        ]
+    )
+
+
+def swapped(block, axis, first):
     count = lax.axis_size(axis)
-    route = [(i, i + distance) for i in range(count) if 0 <= i + distance < count]
-    return lax.ppermute(block, axis, route)
+    route = [(i, i + 1) for i in range(first, count - 1, 2)]
+    return lax.ppermute(block, axis, route + [(j, i) for i, j in route])
 
 
 def local(
@@ -435,50 +465,51 @@
     first_moment,
     second_moment,
 ):
-    vmem, smem = pltpu.VMEM, pltpu.SMEM
+    vmem, dma = pltpu.VMEM, pltpu.SemaphoreType.DMA
     fields = [
         field.reshape(PLANES, ROWS, LANES)
         for field in (electric, magnetic, adjoint_electric, adjoint_magnetic)
     ]
-    xl, xr, dc = call(
-        pack_x_kernel,
-        [f32(X_TILES, ROWS, LANES), f32(X_TILES, ROWS, LANES), f32(2, ROWS, LANES)],
-        (*fields, background, absorb_x, absorb_y.reshape(1, LANES)),
-        [vmem] * 5 + [smem, vmem],
-        "pack_x",
+    sa, x1, x2, planes = call(
+        pack_kernel,
+        [
+            near_by(SHARDS, 2, ROWS, LANES),
+            near_by(X_TILES, ROWS, LANES),
+            near_by(X_TILES, ROWS, LANES),
+            near_by(4 * PLANES + NZ + 2, ROWS, LANES),
+        ],
+        (*fields, background, absorb_x, absorb_y.reshape(1, LANES), design),
         8,
-    )
-    rxl = shifted(xl, "gx", -1)
-    rxr = shifted(xr, "gx", 1)
-    (sa,) = call(
-        pack_design_kernel, [f32(SHARDS, 2, ROWS, LANES)], (design,), [vmem], "pack_design", 4
+        [
+            vmem((DZ, ROWS, LANES), jnp.float32),
+            pltpu.SMEM((ROWS,), jnp.int32),
+            vmem((1, LANES), jnp.int32),
+            dma((8,)),
+        ],
+        far_args=range(8),
     )
     ra = lax.all_to_all(sa, "gx", split_axis=0, concat_axis=0, tiled=True)
-    yl, yr, hx = call(
+    rx1 = swapped(x1, "gx", 0)
+    rx2 = swapped(x2, "gx", 1)
+    (sb,) = call(repack_design_kernel, [near_by(8, 3, 2, ROWS, LANES)], (ra,), 4)
+    rb = lax.all_to_all(sb, "gy", split_axis=0, concat_axis=0, tiled=True)
+    y1, y2, hx = call(
         pack_y_kernel,
         [
-            f32(Y_TILES, ROWS, LANES),
-            f32(Y_TILES, ROWS, LANES),
-            f32(4 * PLANES + NZ + 2, ROWS, LANES),
+            near_by(Y_TILES, ROWS, LANES),
+            near_by(Y_TILES, ROWS, LANES),
+            near_by(4 * PLANES + NZ + 2, ROWS, LANES),
         ],
-        (*fields, background, dc, rxl, rxr),
-        [vmem] * 8,
-        "pack_y",
+        (planes, rx1, rx2),
         8,
     )
-    ryl = shifted(yl, "gy", -1)
-    ryr = shifted(yr, "gy", 1)
-    (sb,) = call(
-        repack_design_kernel, [f32(8, 3, 2, ROWS, LANES)], (ra,), [vmem], "repack_design", 4
-    )
-    rb = lax.all_to_all(sb, "gy", split_axis=0, concat_axis=0, tiled=True)
+    ry1 = swapped(y1, "gy", 0)
+    ry2 = swapped(y2, "gy", 1)
     extended = vmem((3, NZ, 16, 256), jnp.float32)
     eo, ho, go, ko, send = call(
         main_kernel,
-        [f32(PLANES, ROWS, LANES)] * 4 + [f32(128, ROWS, LANES)],
-        (slab_offset, *fields, background, dc, hx, ryl, ryr, rb),
-        [smem] + [vmem] * 10,
-        "time_steps",
+        [f32(PLANES, ROWS, LANES)] * 4 + [near_by(128, ROWS, LANES)],
+        (slab_offset, planes, hx, ry1, ry2, rb),
         24,
         [
             extended,
@@ -495,20 +526,16 @@
             vmem((2, NZ, 16, 256), jnp.float32),
             vmem((3, NZ, 16, 256), jnp.float32),
             vmem((256, 256), jnp.float32),
-            pltpu.SemaphoreType.DMA((12,)),
+            dma((12,)),
         ],
         10,
-        4,
+        scalar_args=(0,),
+        far_outs=range(4),
     )
     arrived = lax.all_to_all(send, ("gx", "gy"), split_axis=0, concat_axis=0, tiled=True)
     shard = f32(DZ, ROWS, LANES)
     design_next, first_next, second_next = call(
-        adam_kernel,
-        [shard] * 3,
-        (arrived, design, first_moment, second_moment),
-        [vmem] * 4,
-        "adam",
-        4,
+        adam_kernel, [shard] * 3, (arrived, design, first_moment, second_moment), 4
     )
     shape = electric.shape
     return (
@@ -527,4 +554,5 @@
     rows = P(None, ("gx", "gy"), None)
     in_specs = (grid, grid, grid, grid, P(None, "gx", "gy"), P("gx"), P("gy"), P(), rows, rows, rows)
     out_specs = (grid, grid, grid, grid, rows, rows, rows)
+
     return jax.shard_map(local, mesh=mesh, in_specs=in_specs, out_specs=out_specs, check_vma=False)

time: 82.8 us -> 74.7 us (0.902)
  local copies, waits for them, and re-layouts: 6.84 us -> 0.02 us
  starting transfers between devices: 17.5 us -> 13.4 us
  blocking collectives: 41.2 us -> 43.3 us
  waiting for transfers between devices: 1.31 us -> 2.78 us
    unnamed x32 -> x6, local copies, waits for them, and re-layouts: 6.84 us -> 0.02 us
    ppermute x4, starting transfers between devices: 13.4 us -> 8.4 us  [swapped(): return lax.ppermute(block, axis, route + [(j, i) for i, j in route])]
    all_to_all x1, waiting for transfers between devices: 0.01 us -> 1.3 us  [local(): rb = lax.all_to_all(sb, 'gy', split_axis=0, concat_axis=0, tiled=True)]
    all_to_all x1, blocking collectives: 25.2 us -> 26.3 us  [local(): lax.all_to_all(send, ('gx', 'gy'), split_axis=0, concat_axis=0, tiled=True)]
    all_to_all x1, blocking collectives: 16 us -> 17 us  [local(): ra = lax.all_to_all(sa, 'gx', split_axis=0, concat_axis=0, tiled=True)]
    all_to_all x1, starting transfers between devices: 4.13 us -> 5.03 us  [local(): rb = lax.all_to_all(sb, 'gy', split_axis=0, concat_axis=0, tiled=True)]
    pallas_call x6 -> x5, Pallas kernels: 13.9 us -> 13.5 us  [call(): pl.pallas_call(kernel, out_shape=outs, in_specs=[pl.BlockSpec(memory_spac...]
  transfers between devices with their start and end apart: 5 -> 5, of which waited for: 2 -> 2; matrix products, arithmetic and copies ran while one was open for 0% -> 0% of each run, Pallas kernels for 4% -> 3%
where the time goes in v2:
time: 74.7 us; the launch traced here: 74.4 us
  blocking collectives  43.3 us (58%)
  Pallas kernels  13.5 us (18%)
  starting transfers between devices  13.4 us (18%)
  waiting for transfers between devices  2.78 us (4%)
  between operations  1.36 us (2%)
    all_to_all x1, blocking collectives, local(): lax.all_to_all(send, ('gx', 'gy'), split_axis=0, concat_axis=0, tiled=True)  26.3 us
    all_to_all x1, blocking collectives, local(): ra = lax.all_to_all(sa, 'gx', split_axis=0, concat_axis=0, tiled=True)  17 us
    pallas_call x5, Pallas kernels, call(): pl.pallas_call(kernel, out_shape=outs, in_specs=[pl.BlockSpec(memory_spac...  13.5 us
    ppermute x4, starting transfers between devices, swapped(): return lax.ppermute(block, axis, route + [(j, i) for i, j in route])  8.4 us
    all_to_all x1, starting transfers between devices, local(): rb = lax.all_to_all(sb, 'gy', split_axis=0, concat_axis=0, tiled=True)  5.03 us
  transfers between devices with their start and end apart: 5, of which 2 were waited for; matrix products, arithmetic and copies ran while one was open for 0% of the time, Pallas kernels for 3%

profile of v2, /device:TPU:1, one launch (start us, length us, event | category | flops | bytes accessed | tf_op | source)
XLA Modules:
  0.0 74.4 jit_solution(15418949270101411026)
XLA Ops:
  0.6 1.7 %shard_map.162 = (f32[16,2,8,128]{3,2,1,0:T(8,128)S(1)}, f32[131,8,128]{2,1,0:T(8,128)S(1)}, f32[131,8,128]{2,1,0:T(8,128)S(1)}, f32[262,8,128]{2,1,0:T(8,128)S(1)}) custom-call(f32[60,8,128]{2,1,0:T(8,128)} %bitcast.9, f32[60,8,128]{2,1,0:T(8,128)} %bitcast.10, f32[60,8,128]{2,1,0:T(8,128)} %bitcast.11, f32[60,8,128]{2,1,0:T(8,128)} %bitcast.12, ...), custom_call_target="tpu_custom_call" | custom-call | flops 1000000 | bytes 1000000 | tf_op jit(solution)/shard_map/pallas_call | solution.py:428
  2.3 1.5 %collective-permute-start = (f32[131,8,128]{2,1,0:T(8,128)S(1)}, f32[131,8,128]{2,1,0:T(8,128)S(1)}, u32[]{:S(2)}, u32[]{:S(2)}) collective-permute-start(f32[131,8,128]{2,1,0:T(8,128)S(1)} %get-tuple-element.23), channel_id=1, source_target_pairs={{0,8},{16,24},{32,40},{48,56},{64,72},{80,88},{96,104},{112,120},{... | collective-permute-start | bytes 1609736 | tf_op jit(solution)/shard_map/ppermute | solution.py:452
  3.8 4.8 %collective-permute-start.1 = (f32[131,8,128]{2,1,0:T(8,128)S(1)}, f32[131,8,128]{2,1,0:T(8,128)S(1)}, u32[]{:S(2)}, u32[]{:S(2)}) collective-permute-start(f32[131,8,128]{2,1,0:T(8,128)S(1)} %get-tuple-element.24), channel_id=1, source_target_pairs={{8,16},{24,32},{40,48},{56,64},{72,80},{88,96},{104,112},{16,8},{3... | collective-permute-start | bytes 1609736 | tf_op jit(solution)/shard_map/ppermute | solution.py:452
  8.6 17.0 %all_to_all.15.ra = f32[16,2,8,128]{3,2,1,0:T(8,128)S(1)} all-to-all(f32[16,2,8,128]{3,2,1,0:T(8,128)S(1)} %get-tuple-element.28), channel_id=1, replica_groups=mesh['gx'=16,'gy'=8] {'gx'}, dimensions={0} | all-to-all | bytes 262144 | tf_op jit(solution)/shard_map/all_to_all | solution.py:491
  25.6 0.7 shard_map.164
  26.3 5.0 %all-to-all-start.1 = ((f32[8,3,2,8,128]{4,3,2,1,0:T(8,128)}), f32[8,3,2,8,128]{4,3,2,1,0:T(8,128)S(1)}, u32[]{:S(2)}, u32[]{:S(2)}) async-start(f32[8,3,2,8,128]{4,3,2,1,0:T(8,128)} %shard_map.164), calls=%async_computation.1 | async-start | bytes 393216 | tf_op jit(solution)/shard_map/all_to_all | solution.py:495
  31.4 0.0 collective-permute-done.rx1
  31.4 0.0 collective-permute-done.1.rx2
  31.4 1.7 %shard_map.163 = (f32[33,8,128]{2,1,0:T(8,128)}, f32[33,8,128]{2,1,0:T(8,128)S(1)}, f32[262,8,128]{2,1,0:T(8,128)S(1)}) custom-call(f32[262,8,128]{2,1,0:T(8,128)S(1)} %get-tuple-element.22.planes, f32[131,8,128]{2,1,0:T(8,128)S(1)} %collective-permute-done.rx1, f32[131,8,128]{2,1,0:T(8,128)S(1)} %collective-permute-done.1.rx2), custom_call_target="tpu_custom_call" | custom-call | flops 1000000 | bytes 1000000 | tf_op jit(solution)/shard_map/pallas_call | solution.py:428
  33.1 1.5 %collective-permute-start.2 = (f32[33,8,128]{2,1,0:T(8,128)}, f32[33,8,128]{2,1,0:T(8,128)S(1)}, u32[]{:S(2)}, u32[]{:S(2)}) collective-permute-start(f32[33,8,128]{2,1,0:T(8,128)} %get-tuple-element.26), channel_id=1, source_target_pairs={{0,1},{2,3},{4,5},{6,7},{1,0},{3,2},{5,4},{7,6},{8,9},{10,11},{12,... | collective-permute-start | bytes 405512 | tf_op jit(solution)/shard_map/ppermute | solution.py:452
  34.5 0.7 collective-permute-start.3
  35.8 1.3 %all-to-all-done.1.rb = f32[8,3,2,8,128]{4,3,2,1,0:T(8,128)S(1)} async-done(((f32[8,3,2,8,128]{4,3,2,1,0:T(8,128)}), f32[8,3,2,8,128]{4,3,2,1,0:T(8,128)S(1)}, u32[]{:S(2)}, u32[]{:S(2)}) %all-to-all-start.1) | async-done | bytes 196640 | tf_op jit(solution)/shard_map/all_to_all | solution.py:495
  37.1 1.5 %collective-permute-done.2.ry1 = f32[33,8,128]{2,1,0:T(8,128)S(1)} collective-permute-done((f32[33,8,128]{2,1,0:T(8,128)}, f32[33,8,128]{2,1,0:T(8,128)S(1)}, u32[]{:S(2)}, u32[]{:S(2)}) %collective-permute-start.2) | collective-permute-done | bytes 135200 | tf_op jit(solution)/shard_map/ppermute | solution.py:452
  38.6 0.0 collective-permute-done.3.ry2
  38.6 7.7 %shard_map.165 = (f32[60,8,128]{2,1,0:T(8,128)}, f32[60,8,128]{2,1,0:T(8,128)}, f32[60,8,128]{2,1,0:T(8,128)}, f32[60,8,128]{2,1,0:T(8,128)}, f32[128,8,128]{2,1,0:T(8,128)S(1)}) custom-call(s32[1]{0:T(128)S(6)} %copy.18.offset_ref, f32[262,8,128]{2,1,0:T(8,128)S(1)} %get-tuple-element.22.planes, f32[262,8,128]{2,1,0:T(8,128)S(1)} %get-tuple-element.25.hx, ...), custom_call_target="tpu_custom_call" | custom-call | flops 10000000 | bytes 10000000 | tf_op jit(solution)/shard_map/pallas_call | solution.py:428
  46.3 0.0 copy-start
  46.4 0.0 copy-start.1
  46.4 0.0 copy-start.2
  46.4 26.3 %all_to_all.16.arrived = f32[128,8,128]{2,1,0:T(8,128)S(1)} all-to-all(f32[128,8,128]{2,1,0:T(8,128)S(1)} %get-tuple-element.33), channel_id=1, replica_groups=mesh['gx'=16,'gy'=8] {'gx','gy'}, dimensions={0} | all-to-all | bytes 1048576 | tf_op jit(solution)/shard_map/all_to_all | solution.py:535
  72.7 0.0 copy-done
  72.7 0.0 copy-done.1
  72.7 0.0 copy-done.2
  72.7 1.7 %shard_map.166 = (f32[16,8,128]{2,1,0:T(8,128)}, f32[16,8,128]{2,1,0:T(8,128)}, f32[16,8,128]{2,1,0:T(8,128)}) custom-call(f32[128,8,128]{2,1,0:T(8,128)S(1)} %all_to_all.16.arrived, f32[16,8,128]{2,1,0:T(8,128)S(1)} %copy-done, f32[16,8,128]{2,1,0:T(8,128)S(1)} %copy-done.1, f32[16,8,128]{2,1,0:T(8,128)S(1)} %copy-done.2), custom_call_target="tpu_custom_call" | custom-call | flops 1000000 | bytes 1000000 | tf_op jit(solution)/shard_map/pallas_call | solution.py:428
Async XLA Ops:
  2.3 29.1 %collective-permute-start = (f32[131,8,128]{2,1,0:T(8,128)S(1)}, f32[131,8,128]{2,1,0:T(8,128)S(1)}, u32[]{:S(2)}, u32[]{:S(2)}) collective-permute-start(f32[131,8,128]{2,1,0:T(8,128)S(1)} %get-tuple-element.23), channel_id=1, source_target_pairs={{0,8},{16,24},{32,40},{48,56},{64,72},{80,88},{96,104},{112,120},{... | collective-permute-start | bytes 1609736 | tf_op jit(solution)/shard_map/ppermute | solution.py:452
  3.8 27.6 %collective-permute-start.1 = (f32[131,8,128]{2,1,0:T(8,128)S(1)}, f32[131,8,128]{2,1,0:T(8,128)S(1)}, u32[]{:S(2)}, u32[]{:S(2)}) collective-permute-start(f32[131,8,128]{2,1,0:T(8,128)S(1)} %get-tuple-element.24), channel_id=1, source_target_pairs={{8,16},{24,32},{40,48},{56,64},{72,80},{88,96},{104,112},{16,8},{3... | collective-permute-start | bytes 1609736 | tf_op jit(solution)/shard_map/ppermute | solution.py:452
  26.3 10.8 %all-to-all-start.1 = ((f32[8,3,2,8,128]{4,3,2,1,0:T(8,128)}), f32[8,3,2,8,128]{4,3,2,1,0:T(8,128)S(1)}, u32[]{:S(2)}, u32[]{:S(2)}) async-start(f32[8,3,2,8,128]{4,3,2,1,0:T(8,128)} %shard_map.164), calls=%async_computation.1 | async-start | bytes 393216 | tf_op jit(solution)/shard_map/all_to_all | solution.py:495
  33.1 5.5 %collective-permute-start.2 = (f32[33,8,128]{2,1,0:T(8,128)}, f32[33,8,128]{2,1,0:T(8,128)S(1)}, u32[]{:S(2)}, u32[]{:S(2)}) collective-permute-start(f32[33,8,128]{2,1,0:T(8,128)} %get-tuple-element.26), channel_id=1, source_target_pairs={{0,1},{2,3},{4,5},{6,7},{1,0},{3,2},{5,4},{7,6},{8,9},{10,11},{12,... | collective-permute-start | bytes 405512 | tf_op jit(solution)/shard_map/ppermute | solution.py:452
  34.5 4.1 %collective-permute-start.3 = (f32[33,8,128]{2,1,0:T(8,128)S(1)}, f32[33,8,128]{2,1,0:T(8,128)S(1)}, u32[]{:S(2)}, u32[]{:S(2)}) collective-permute-start(f32[33,8,128]{2,1,0:T(8,128)S(1)} %get-tuple-element.27), channel_id=1, source_target_pairs={{1,2},{3,4},{5,6},{2,1},{4,3},{6,5},{9,10},{11,12},{13,14},{10,9},... | collective-permute-start | bytes 405512 | tf_op jit(solution)/shard_map/ppermute | solution.py:452
  46.3 26.3 %copy-start = (f32[16,8,128]{2,1,0:T(8,128)S(1)}, f32[16,8,128]{2,1,0:T(8,128)}, u32[]{:S(2)}) copy-start(f32[16,8,128]{2,1,0:T(8,128)} %design.3) | copy-start | bytes 196612
  46.4 26.3 %copy-start.1 = (f32[16,8,128]{2,1,0:T(8,128)S(1)}, f32[16,8,128]{2,1,0:T(8,128)}, u32[]{:S(2)}) copy-start(f32[16,8,128]{2,1,0:T(8,128)} %first.1) | copy-start | bytes 196612
  46.4 26.3 %copy-start.2 = (f32[16,8,128]{2,1,0:T(8,128)S(1)}, f32[16,8,128]{2,1,0:T(8,128)}, u32[]{:S(2)}) copy-start(f32[16,8,128]{2,1,0:T(8,128)} %second.1) | copy-start | bytes 196612

commit v3 on v2

--- a/solution.py
+++ b/solution.py
@@ -30,9 +30,10 @@
 LANES = 128
 SHARDS = 16
 PLANES = 3 * NZ
-FIELD_TILES = PLANES // 2
-X_TILES = 4 * FIELD_TILES + NZ // 2 + 1
-Y_TILES = 33
+COUNT = 4 * PLANES + NZ + 2
+CORNERS = 34
+X_TILES = COUNT // 2
+Y_TILES = 17
 
 
 def gauss_taps(radius):
@@ -66,10 +67,17 @@
     return lax.broadcasted_iota(jnp.int32, shape, 0), lax.broadcasted_iota(jnp.int32, shape, 1)
 
 
+def pair_rows(first, second, low, turned, x1, x2, tile):
+    before = jnp.where(low, first, roll(second, 4, 0))
+    after = jnp.where(low, roll(first, 4, 0), second)
+    x1[tile] = jnp.where(turned, before, after)
+    x2[tile] = jnp.where(turned, after, before)
+
+
 def pack_kernel(
     e, h, g, k, bg, absorb_x, absorb_y, design,
-    out, x1, x2, planes,
-    rows_ref, level_x_ref, level_y_ref, sems,
+    out, x1, x2, y1, y2, dc,
+    planes, chunks, rows_ref, level_x_ref, level_y_ref, sems,
 ):
     loads = [
         pltpu.make_async_copy(design, rows_ref, sems.at[0]),
@@ -83,7 +91,6 @@
     for load in loads:
         load.start()
     row, lane = iotas()
-    low = row < 4
 
     group = lane // 16
     loads[0].wait()
@@ -93,7 +100,9 @@
             total = roll(rows[0], 4 - 8 * a, 1)
             for kk in range(1, 8):
                 total = jnp.where(group == kk, roll(rows[kk], 16 * kk + 4 - 8 * a, 1), total)
-            out[a, kh] = total
+            chunks[a, kh] = total
+    leave = pltpu.make_async_copy(chunks, out, sems.at[8])
+    leave.start()
 
     loads[1].wait()
     loads[2].wait()
@@ -103,81 +112,57 @@
     level_x = level_x / PML_DEPTH
     level_y = jnp.broadcast_to(level_y_ref[...].astype(jnp.float32) / PML_DEPTH, (ROWS, LANES))
     damping = SIGMA_MAX * (level_x * level_x + level_y * level_y)
-    planes[4 * PLANES + NZ] = (1.0 - damping) / (1.0 + damping)
-    planes[4 * PLANES + NZ + 1] = COURANT / (1.0 + damping)
-
-    turned = lax.axis_index("gx") % 2 == 1
-
-    def pair(index):
-        first, second = planes[2 * index], planes[2 * index + 1]
-        before = jnp.where(low, first, roll(second, 4, 0))
-        after = jnp.where(low, roll(first, 4, 0), second)
-        x1[index] = jnp.where(turned, before, after)
-        x2[index] = jnp.where(turned, after, before)
-
-    for number in range(4):
-        loads[3 + number].wait()
-        for i in range(FIELD_TILES):
-            pair(number * FIELD_TILES + i)
-    loads[7].wait()
-    for i in range(NZ // 2 + 1):
-        pair(4 * FIELD_TILES + i)
-
-
-def pack_y_kernel(planes, rx1, rx2, y1, y2, hx):
+    decay = (1.0 - damping) / (1.0 + damping)
+    coupling = COURANT / (1.0 + damping)
+    for i, values in enumerate((decay, coupling)):
+        planes[4 * PLANES + NZ + i] = values
+        dc[i] = values
+
+    turned = lax.axis_index("gy") % 2 == 1
+    turned_x = lax.axis_index("gx") % 2 == 1
+    low = row < 4
+    arrived = 0
+    group = lane // 8
+    for m in range(Y_TILES):
+        while arrived < 5 and min(16 * m + 16, 4 * PLANES + NZ) > arrived * PLANES:
+            loads[3 + arrived].wait()
+            arrived += 1
+        before = after = None
+        for j in range(16):
+            if 16 * m + j >= COUNT:
+                continue
+            moved = roll(planes[16 * m + j], 8 * j, 1)
+            before = moved if j == 0 else jnp.where(group == j, moved, before)
+            after = moved if j == 0 else jnp.where(group == (j - 1) % 16, moved, after)
+        y1[m] = jnp.where(turned, before, after)
+        y2[m] = jnp.where(turned, after, before)
+        for tile in range(8 * m, min(8 * m + 8, X_TILES)):
+            pair_rows(planes[2 * tile], planes[2 * tile + 1], low, turned_x, x1, x2, tile)
+    leave.wait()
+
+
+def pack_corner_kernel(ry1, ry2, c1, c2, corner):
     row, lane = iotas()
     low = row < 4
-    group = lane // 8
-
+    even = (lane // 8) % 2 == 0
     turned_x = lax.axis_index("gx") % 2 == 1
     turned_y = lax.axis_index("gy") % 2 == 1
 
-    def halo(tile, odd):
-        after = jnp.where(turned_x, rx2[tile], rx1[tile])
-        before = jnp.where(turned_x, rx1[tile], rx2[tile])
-        if odd:
-            return jnp.where(low, roll(after, 4, 0), before)
-        return jnp.where(low, after, roll(before, 4, 0))
-
-    def send(index, before, after):
-        y1[index] = jnp.where(turned_y, before, after)
-        y2[index] = jnp.where(turned_y, after, before)
-
-    def put(totals, values, j):
-        moved = roll(values, 8 * j, 1)
-        if totals is None:
-            return moved, moved
-        before = (j - 1) % 16
-        return jnp.where(group == j, moved, totals[0]), jnp.where(group == before, moved, totals[1])
-
-    for half in range(2):
-
-        def body(c, carry):
-            for n in range(5):
-                i = 5 * c + n
-                totals = None
-                for number in range(2):
-                    which = 2 * half + number
-                    for q in range(4):
-                        edge = halo(which * FIELD_TILES + 2 * i + q // 2, q % 2)
-                        hx[which * PLANES + 4 * i + q] = edge
-                        totals = put(totals, planes[which * PLANES + 4 * i + q], 8 * number + 2 * q)
-                        totals = put(totals, edge, 8 * number + 2 * q + 1)
-                send(15 * half + i, *totals)
-            return carry
-
-        lax.fori_loop(0, 3, body, 0)
-    for m in range(3):
-        totals = None
-        for q in range(8):
-            p = 8 * m + q
-            if p >= NZ + 2:
-                continue
-            edge = halo(4 * FIELD_TILES + p // 2, p % 2)
-            hx[4 * PLANES + p] = edge
-            totals = put(totals, planes[4 * PLANES + p], 2 * q)
-            totals = put(totals, edge, 2 * q + 1)
-        send(30 + m, *totals)
+    for m in range(Y_TILES):
+        after = jnp.where(turned_y, ry2[m], ry1[m])
+        before = jnp.where(turned_y, ry1[m], ry2[m])
+        mixed = jnp.where(even, after, before), jnp.where(even, before, after)
+        for half in range(2):
+            total = jnp.zeros((ROWS, LANES), jnp.float32)
+            for q in range(8):
+                j = 8 * half + q
+                if 16 * m + j >= COUNT:
+                    continue
+                moved = roll(mixed[j % 2], 16 * q + 8 - 8 * j, 1)
+                total = jnp.where(lane // 16 == q, moved, total)
+            corner[2 * m + half] = total
+    for m in range(CORNERS // 2):
+        pair_rows(corner[2 * m], corner[2 * m + 1], low, turned_x, c1, c2, m)
 
 
 def repack_design_kernel(ra, sb):
@@ -191,54 +176,60 @@
 
 
 def main_kernel(
-    offset_ref, planes, hx, ry1, ry2, rb,
+    offset_ref, e, h, g, k, bg, dc, ry1, ry2, rx1, rx2, rc1, rc2, rb,
     eo, ho, go, ko, send,
     es, hs, gs, ks, gain, dcy, cpl, dx, ch, sn, sf, rot, ws, band, sems,
 ):
     b = lax.axis_index("gy")
-    _, lane = iotas()
+    row, lane = iotas()
+    low = row < 4
     group = lane // 8
     even = group % 2 == 0
     edges = (group == 0) | (group == 15)
+    turned = lax.axis_index("gx") % 2 == 1
+    turned_y = b % 2 == 1
     top, bottom = pl.ds(0, 8), pl.ds(8, 8)
     near, far = pl.ds(0, 128), pl.ds(128, 128)
 
-    turned_y = b % 2 == 1
-
-    def sides(m):
+    loads = [pltpu.make_async_copy(bg, gain.at[:, top, near], sems.at[24])]
+    for number, (field, ext) in enumerate(((e, es), (h, hs), (g, gs), (k, ks))):
+        for c in range(3):
+            source = field.at[pl.ds(c * NZ, NZ)]
+            slot = sems.at[12 + 3 * number + c]
+            loads.append(pltpu.make_async_copy(source, ext.at[c, :, top, near], slot))
+    for load in loads:
+        load.start()
+
+    def halos(r1, r2, tile):
+        after = jnp.where(turned, r2[tile], r1[tile])
+        before = jnp.where(turned, r1[tile], r2[tile])
+        return (
+            jnp.where(low, after, roll(before, 4, 0)),
+            jnp.where(low, roll(after, 4, 0), before),
+        )
+
+    targets = [ext.at[c, z] for ext in (es, hs, gs, ks) for c in range(3) for z in range(NZ)]
+    targets += [gain.at[z] for z in range(NZ)] + [dcy, cpl]
+    for m in range(CORNERS // 2):
+        corners = halos(rc1, rc2, m)
         after = jnp.where(turned_y, ry2[m], ry1[m])
         before = jnp.where(turned_y, ry1[m], ry2[m])
         mixed = jnp.where(even, after, before), jnp.where(even, before, after)
-        return lambda j: jnp.where(edges, roll(mixed[j % 2], -8 * j, 1), 0.0)
-
-    for half, pairs in enumerate(((es, hs), (gs, ks))):
-
-        def unpack(c, carry):
-            for i in range(5):
-                side = sides(15 * half + 5 * c + i)
-                for number, ext in enumerate(pairs):
-                    which = 2 * half + number
-                    for q in range(4):
-                        z = 4 * i + q
-                        j = 8 * number + 2 * q
-                        ext[c, z, top, near] = planes[which * PLANES + c * NZ + z]
-                        ext[c, z, bottom, near] = hx[which * PLANES + c * NZ + z]
-                        ext[c, z, top, far] = side(j)
-                        ext[c, z, bottom, far] = side(j + 1)
-            return carry
-
-        lax.fori_loop(0, 3, unpack, 0)
-    for m in range(3):
-        side = sides(30 + m)
-        for q in range(8):
-            p = 8 * m + q
-            if p >= NZ + 2:
+        for half in range(8):
+            p = 16 * m + 2 * half
+            if p >= COUNT:
                 continue
-            ext = gain.at[p] if p < NZ else (dcy, cpl)[p - NZ]
-            ext[top, near] = planes[4 * PLANES + p]
-            ext[bottom, near] = hx[4 * PLANES + p]
-            ext[top, far] = side(2 * q)
-            ext[bottom, far] = side(2 * q + 1)
+            edge = halos(rx1, rx2, p // 2)
+            for odd in range(2):
+                q = (2 * half + odd) % 8
+                ext = targets[p + odd]
+                if p >= 4 * PLANES + NZ:
+                    ext[top, near] = dc[odd]
+                ext[bottom, near] = edge[odd]
+                j = 2 * half + odd
+                ext[top, far] = jnp.where(edges, roll(mixed[odd], -8 * j, 1), 0.0)
+                moved = roll(corners[half // 4], -16 * q - 8, 1)
+                ext[bottom, far] = jnp.where(edges, moved, 0.0)
     plane = jnp.zeros((16, 256), jnp.float32)
 
     shape = (256, 256)
@@ -266,6 +257,7 @@
             dx[8 * kh + kk] = roll(smooth[16 * kk:16 * kk + 16], -4, 0)
 
     edge = math.tanh(SHARPNESS * THRESHOLD)
+    loads[0].wait()
     offset = offset_ref[0]
 
     def project(layer, carry):
@@ -328,6 +320,8 @@
                 es[c, z] = decay * es[c, z] + rate * back[c]
         return carry
 
+    for load in loads[1:7]:
+        load.wait()
     lax.fori_loop(0, STEPS, forward, 0)
     copies = []
 
@@ -371,6 +365,8 @@
                 gs[c, z] = decay * gs[c, z] - back[c]
         return carry
 
+    for load in loads[7:]:
+        load.wait()
     lax.fori_loop(0, STEPS, backward, 0)
     export(gs, go, 2)
     export(ks, ko, 3)
@@ -470,46 +466,50 @@
         field.reshape(PLANES, ROWS, LANES)
         for field in (electric, magnetic, adjoint_electric, adjoint_magnetic)
     ]
-    sa, x1, x2, planes = call(
+    sa, x1, x2, y1, y2, dc = call(
         pack_kernel,
         [
-            near_by(SHARDS, 2, ROWS, LANES),
+            f32(SHARDS, 2, ROWS, LANES),
             near_by(X_TILES, ROWS, LANES),
             near_by(X_TILES, ROWS, LANES),
-            near_by(4 * PLANES + NZ + 2, ROWS, LANES),
+            near_by(Y_TILES, ROWS, LANES),
+            near_by(Y_TILES, ROWS, LANES),
+            near_by(2, ROWS, LANES),
         ],
         (*fields, background, absorb_x, absorb_y.reshape(1, LANES), design),
         8,
         [
+            vmem((COUNT, ROWS, LANES), jnp.float32),
+            vmem((SHARDS, 2, ROWS, LANES), jnp.float32),
             vmem((DZ, ROWS, LANES), jnp.float32),
             pltpu.SMEM((ROWS,), jnp.int32),
             vmem((1, LANES), jnp.int32),
-            dma((8,)),
+            dma((9,)),
         ],
         far_args=range(8),
-    )
-    ra = lax.all_to_all(sa, "gx", split_axis=0, concat_axis=0, tiled=True)
+        far_outs=(0,),
+    )
     rx1 = swapped(x1, "gx", 0)
     rx2 = swapped(x2, "gx", 1)
+    ry1 = swapped(y1, "gy", 0)
+    ry2 = swapped(y2, "gy", 1)
+    ra = lax.all_to_all(sa, "gx", split_axis=0, concat_axis=0, tiled=True)
+    c1, c2 = call(
+        pack_corner_kernel,
+        [near_by(CORNERS // 2, ROWS, LANES)] * 2,
+        (ry1, ry2),
+        4,
+        [vmem((CORNERS, ROWS, LANES), jnp.float32)],
+    )
+    rc1 = swapped(c1, "gx", 0)
+    rc2 = swapped(c2, "gx", 1)
     (sb,) = call(repack_design_kernel, [near_by(8, 3, 2, ROWS, LANES)], (ra,), 4)
     rb = lax.all_to_all(sb, "gy", split_axis=0, concat_axis=0, tiled=True)
-    y1, y2, hx = call(
-        pack_y_kernel,
-        [
-            near_by(Y_TILES, ROWS, LANES),
-            near_by(Y_TILES, ROWS, LANES),
-            near_by(4 * PLANES + NZ + 2, ROWS, LANES),
-        ],
-        (planes, rx1, rx2),
-        8,
-    )
-    ry1 = swapped(y1, "gy", 0)
-    ry2 = swapped(y2, "gy", 1)
     extended = vmem((3, NZ, 16, 256), jnp.float32)
     eo, ho, go, ko, send = call(
         main_kernel,
         [f32(PLANES, ROWS, LANES)] * 4 + [near_by(128, ROWS, LANES)],
-        (slab_offset, planes, hx, ry1, ry2, rb),
+        (slab_offset, *fields, background, dc, ry1, ry2, rx1, rx2, rc1, rc2, rb),
         24,
         [
             extended,
@@ -526,9 +526,10 @@
             vmem((2, NZ, 16, 256), jnp.float32),
             vmem((3, NZ, 16, 256), jnp.float32),
             vmem((256, 256), jnp.float32),
-            dma((12,)),
+            dma((25,)),
         ],
         10,
+        far_args=range(1, 6),
         scalar_args=(0,),
         far_outs=range(4),
     )

time: 74.7 us -> 81.4 us (1.090)
  starting transfers between devices: 13.4 us -> 20.5 us
  waiting for transfers between devices: 2.78 us -> 4.45 us
  blocking collectives: 43.3 us -> 42 us
  Pallas kernels: 13.5 us -> 12.6 us
    ppermute x4 -> x6, starting transfers between devices: 8.4 us -> 15.5 us  [swapped(): return lax.ppermute(block, axis, route + [(j, i) for i, j in route])]
    ppermute x4 -> x6, waiting for transfers between devices: 1.47 us -> 4.45 us  [swapped(): return lax.ppermute(block, axis, route + [(j, i) for i, j in route])]
    all_to_all x1, waiting for transfers between devices: 1.3 us -> 0.01 us  [local(): rb = lax.all_to_all(sb, 'gy', split_axis=0, concat_axis=0, tiled=True)]
    all_to_all x1, blocking collectives: 26.3 us -> 25 us  [local(): lax.all_to_all(send, ('gx', 'gy'), split_axis=0, concat_axis=0, tiled=True)]
    pallas_call x5, Pallas kernels: 13.5 us -> 12.6 us  [call(): pl.pallas_call(kernel, out_shape=outs, in_specs=[pl.BlockSpec(memory_spac...]
  transfers between devices with their start and end apart: 5 -> 7, of which waited for: 2 -> 2; matrix products, arithmetic and copies ran while one was open for 0% -> 0% of each run, Pallas kernels for 3% -> 1%
where the time goes in v3:
time: 81.4 us; the launch traced here: 81 us
  blocking collectives  42 us (52%)
  starting transfers between devices  20.5 us (25%)
  Pallas kernels  12.6 us (15%)
  waiting for transfers between devices  4.45 us (5%)
  between operations  1.37 us (2%)
    all_to_all x1, blocking collectives, local(): lax.all_to_all(send, ('gx', 'gy'), split_axis=0, concat_axis=0, tiled=True)  25 us
    all_to_all x1, blocking collectives, local(): ra = lax.all_to_all(sa, 'gx', split_axis=0, concat_axis=0, tiled=True)  17 us
    ppermute x6, starting transfers between devices, swapped(): return lax.ppermute(block, axis, route + [(j, i) for i, j in route])  15.5 us
    pallas_call x5, Pallas kernels, call(): pl.pallas_call(kernel, out_shape=outs, in_specs=[pl.BlockSpec(memory_spac...  12.6 us
    all_to_all x1, starting transfers between devices, local(): rb = lax.all_to_all(sb, 'gy', split_axis=0, concat_axis=0, tiled=True)  5.03 us
    ppermute x6, waiting for transfers between devices, swapped(): return lax.ppermute(block, axis, route + [(j, i) for i, j in route])  4.45 us
  transfers between devices with their start and end apart: 7, of which 2 were waited for; matrix products, arithmetic and copies ran while one was open for 0% of the time, Pallas kernels for 1%

profile of v3, /device:TPU:1, one launch (start us, length us, event | category | flops | bytes accessed | tf_op | source)
XLA Modules:
  0.0 81.0 jit_solution(12856153933665147082)
XLA Ops:
  0.6 2.3 %shard_map.162 = (f32[16,2,8,128]{3,2,1,0:T(8,128)S(1)}, f32[131,8,128]{2,1,0:T(8,128)S(1)}, f32[131,8,128]{2,1,0:T(8,128)S(1)}, f32[17,8,128]{2,1,0:T(8,128)S(1...) custom-call(f32[60,8,128]{2,1,0:T(8,128)} %bitcast.9, f32[60,8,128]{2,1,0:T(8,128)} %bitcast.11, ...), custom_call_target="tpu_custom_call" | custom-call | flops 1000000 | bytes 1000000 | tf_op jit(solution)/shard_map/pallas_call | solution.py:424
  3.0 1.5 %collective-permute-start.2 = (f32[131,8,128]{2,1,0:T(8,128)S(1)}, f32[131,8,128]{2,1,0:T(8,128)S(1)}, u32[]{:S(2)}, u32[]{:S(2)}) collective-permute-start(f32[131,8,128]{2,1,0:T(8,128)S(1)} %get-tuple-element.26), channel_id=1, source_target_pairs={{0,8},{16,24},{32,40},{48,56},{64,72},{80,88},{96,104},{112,120},{... | collective-permute-start | bytes 1609736 | tf_op jit(solution)/shard_map/ppermute | solution.py:448
  4.4 4.8 %collective-permute-start.3 = (f32[131,8,128]{2,1,0:T(8,128)S(1)}, f32[131,8,128]{2,1,0:T(8,128)S(1)}, u32[]{:S(2)}, u32[]{:S(2)}) collective-permute-start(f32[131,8,128]{2,1,0:T(8,128)S(1)} %get-tuple-element.27), channel_id=1, source_target_pairs={{8,16},{24,32},{40,48},{56,64},{72,80},{88,96},{104,112},{16,8},{3... | collective-permute-start | bytes 1609736 | tf_op jit(solution)/shard_map/ppermute | solution.py:448
  9.3 17.0 %all_to_all.15.ra = f32[16,2,8,128]{3,2,1,0:T(8,128)S(1)} all-to-all(f32[16,2,8,128]{3,2,1,0:T(8,128)S(1)} %get-tuple-element.30), channel_id=1, replica_groups=mesh['gx'=16,'gy'=8] {'gx'}, dimensions={0} | all-to-all | bytes 262144 | tf_op jit(solution)/shard_map/all_to_all | solution.py:496
  26.3 0.7 shard_map.164
  27.0 5.0 %all-to-all-start.1 = ((f32[8,3,2,8,128]{4,3,2,1,0:T(8,128)}), f32[8,3,2,8,128]{4,3,2,1,0:T(8,128)S(1)}, u32[]{:S(2)}, u32[]{:S(2)}) async-start(f32[8,3,2,8,128]{4,3,2,1,0:T(8,128)} %shard_map.164), calls=%async_computation.1 | async-start | bytes 393216 | tf_op jit(solution)/shard_map/all_to_all | solution.py:507
  32.0 1.5 %collective-permute-start = (f32[17,8,128]{2,1,0:T(8,128)S(1)}, f32[17,8,128]{2,1,0:T(8,128)S(1)}, u32[]{:S(2)}, u32[]{:S(2)}) collective-permute-start(f32[17,8,128]{2,1,0:T(8,128)S(1)} %get-tuple-element.24), channel_id=1, source_target_pairs={{0,1},{2,3},{4,5},{6,7},{1,0},{3,2},{5,4},{7,6},{8,9},{10,11},{12,... | collective-permute-start | bytes 208904 | tf_op jit(solution)/shard_map/ppermute | solution.py:448
  33.5 0.7 collective-permute-start.1
  34.1 2.3 %collective-permute-done.ry1 = f32[17,8,128]{2,1,0:T(8,128)S(1)} collective-permute-done((f32[17,8,128]{2,1,0:T(8,128)S(1)}, f32[17,8,128]{2,1,0:T(8,128)S(1)}, u32[]{:S(2)}, u32[]{:S(2)}) %collective-permute-start) | collective-permute-done | bytes 69664 | tf_op jit(solution)/shard_map/ppermute | solution.py:448
  36.4 0.0 collective-permute-done.1.ry2
  36.4 0.3 shard_map.163
  36.8 2.8 %collective-permute-start.4 = (f32[17,8,128]{2,1,0:T(8,128)S(1)}, f32[17,8,128]{2,1,0:T(8,128)S(1)}, u32[]{:S(2)}, u32[]{:S(2)}) collective-permute-start(f32[17,8,128]{2,1,0:T(8,128)S(1)} %get-tuple-element.28), channel_id=1, source_target_pairs={{0,8},{16,24},{32,40},{48,56},{64,72},{80,88},{96,104},{112,120},{... | collective-permute-start | bytes 208904 | tf_op jit(solution)/shard_map/ppermute | solution.py:448
  39.6 4.3 %collective-permute-start.5 = (f32[17,8,128]{2,1,0:T(8,128)S(1)}, f32[17,8,128]{2,1,0:T(8,128)S(1)}, u32[]{:S(2)}, u32[]{:S(2)}) collective-permute-start(f32[17,8,128]{2,1,0:T(8,128)S(1)} %get-tuple-element.29), channel_id=1, source_target_pairs={{8,16},{24,32},{40,48},{56,64},{72,80},{88,96},{104,112},{16,8},{3... | collective-permute-start | bytes 208904 | tf_op jit(solution)/shard_map/ppermute | solution.py:448
  44.5 0.0 collective-permute-done.4.rc1
  44.5 2.1 %collective-permute-done.5.rc2 = f32[17,8,128]{2,1,0:T(8,128)S(1)} collective-permute-done((f32[17,8,128]{2,1,0:T(8,128)S(1)}, f32[17,8,128]{2,1,0:T(8,128)S(1)}, u32[]{:S(2)}, u32[]{:S(2)}) %collective-permute-start.5) | collective-permute-done | bytes 69664 | tf_op jit(solution)/shard_map/ppermute | solution.py:448
  46.7 0.0 all-to-all-done.1.rb
  46.7 0.0 collective-permute-done.2.rx1
  46.7 0.0 collective-permute-done.3.rx2
  46.7 7.5 %shard_map.165 = (f32[60,8,128]{2,1,0:T(8,128)}, f32[60,8,128]{2,1,0:T(8,128)}, f32[60,8,128]{2,1,0:T(8,128)}, f32[60,8,128]{2,1,0:T(8,128)}, f32[128,8,128]{2,1,0:T(8,128)S(1)}) custom-call(s32[1]{0:T(128)S(6)} %copy.18.offset_ref, f32[60,8,128]{2,1,0:T(8,128)} %bitcast.10, f32[60,8,128]{2,1,0:T(8,128)} %bitcast.12, f32[60,8,128]{2,1,0:T(8,128)} %bitcast.14, ...), custom_call_target="tpu_custom_call" | custom-call | flops 10000000 | bytes 10000000 | tf_op jit(solution)/shard_map/pallas_call | solution.py:424
  54.2 0.0 copy-start
  54.2 0.0 copy-start.1
  54.2 0.0 copy-start.2
  54.2 25.0 %all_to_all.16.arrived = f32[128,8,128]{2,1,0:T(8,128)S(1)} all-to-all(f32[128,8,128]{2,1,0:T(8,128)S(1)} %get-tuple-element.35), channel_id=1, replica_groups=mesh['gx'=16,'gy'=8] {'gx','gy'}, dimensions={0} | all-to-all | bytes 1048576 | tf_op jit(solution)/shard_map/all_to_all | solution.py:536
  79.2 0.0 copy-done
  79.2 0.0 copy-done.1
  79.2 0.0 copy-done.2
  79.2 1.7 %shard_map.166 = (f32[16,8,128]{2,1,0:T(8,128)}, f32[16,8,128]{2,1,0:T(8,128)}, f32[16,8,128]{2,1,0:T(8,128)}) custom-call(f32[128,8,128]{2,1,0:T(8,128)S(1)} %all_to_all.16.arrived, f32[16,8,128]{2,1,0:T(8,128)S(1)} %copy-done, f32[16,8,128]{2,1,0:T(8,128)S(1)} %copy-done.1, f32[16,8,128]{2,1,0:T(8,128)S(1)} %copy-done.2), custom_call_target="tpu_custom_call" | custom-call | flops 1000000 | bytes 1000000 | tf_op jit(solution)/shard_map/pallas_call | solution.py:424
Async XLA Ops:
  3.0 43.7 %collective-permute-start.2 = (f32[131,8,128]{2,1,0:T(8,128)S(1)}, f32[131,8,128]{2,1,0:T(8,128)S(1)}, u32[]{:S(2)}, u32[]{:S(2)}) collective-permute-start(f32[131,8,128]{2,1,0:T(8,128)S(1)} %get-tuple-element.26), channel_id=1, source_target_pairs={{0,8},{16,24},{32,40},{48,56},{64,72},{80,88},{96,104},{112,120},{... | collective-permute-start | bytes 1609736 | tf_op jit(solution)/shard_map/ppermute | solution.py:448
  4.4 42.3 %collective-permute-start.3 = (f32[131,8,128]{2,1,0:T(8,128)S(1)}, f32[131,8,128]{2,1,0:T(8,128)S(1)}, u32[]{:S(2)}, u32[]{:S(2)}) collective-permute-start(f32[131,8,128]{2,1,0:T(8,128)S(1)} %get-tuple-element.27), channel_id=1, source_target_pairs={{8,16},{24,32},{40,48},{56,64},{72,80},{88,96},{104,112},{16,8},{3... | collective-permute-start | bytes 1609736 | tf_op jit(solution)/shard_map/ppermute | solution.py:448
  27.0 19.7 %all-to-all-start.1 = ((f32[8,3,2,8,128]{4,3,2,1,0:T(8,128)}), f32[8,3,2,8,128]{4,3,2,1,0:T(8,128)S(1)}, u32[]{:S(2)}, u32[]{:S(2)}) async-start(f32[8,3,2,8,128]{4,3,2,1,0:T(8,128)} %shard_map.164), calls=%async_computation.1 | async-start | bytes 393216 | tf_op jit(solution)/shard_map/all_to_all | solution.py:507
  32.0 4.4 %collective-permute-start = (f32[17,8,128]{2,1,0:T(8,128)S(1)}, f32[17,8,128]{2,1,0:T(8,128)S(1)}, u32[]{:S(2)}, u32[]{:S(2)}) collective-permute-start(f32[17,8,128]{2,1,0:T(8,128)S(1)} %get-tuple-element.24), channel_id=1, source_target_pairs={{0,1},{2,3},{4,5},{6,7},{1,0},{3,2},{5,4},{7,6},{8,9},{10,11},{12,... | collective-permute-start | bytes 208904 | tf_op jit(solution)/shard_map/ppermute | solution.py:448
  33.5 3.0 %collective-permute-start.1 = (f32[17,8,128]{2,1,0:T(8,128)S(1)}, f32[17,8,128]{2,1,0:T(8,128)S(1)}, u32[]{:S(2)}, u32[]{:S(2)}) collective-permute-start(f32[17,8,128]{2,1,0:T(8,128)S(1)} %get-tuple-element.25), channel_id=1, source_target_pairs={{1,2},{3,4},{5,6},{2,1},{4,3},{6,5},{9,10},{11,12},{13,14},{10,9},... | collective-permute-start | bytes 208904 | tf_op jit(solution)/shard_map/ppermute | solution.py:448
  36.8 7.7 %collective-permute-start.4 = (f32[17,8,128]{2,1,0:T(8,128)S(1)}, f32[17,8,128]{2,1,0:T(8,128)S(1)}, u32[]{:S(2)}, u32[]{:S(2)}) collective-permute-start(f32[17,8,128]{2,1,0:T(8,128)S(1)} %get-tuple-element.28), channel_id=1, source_target_pairs={{0,8},{16,24},{32,40},{48,56},{64,72},{80,88},{96,104},{112,120},{... | collective-permute-start | bytes 208904 | tf_op jit(solution)/shard_map/ppermute | solution.py:448
  39.6 7.1 %collective-permute-start.5 = (f32[17,8,128]{2,1,0:T(8,128)S(1)}, f32[17,8,128]{2,1,0:T(8,128)S(1)}, u32[]{:S(2)}, u32[]{:S(2)}) collective-permute-start(f32[17,8,128]{2,1,0:T(8,128)S(1)} %get-tuple-element.29), channel_id=1, source_target_pairs={{8,16},{24,32},{40,48},{56,64},{72,80},{88,96},{104,112},{16,8},{3... | collective-permute-start | bytes 208904 | tf_op jit(solution)/shard_map/ppermute | solution.py:448
  54.2 25.1 %copy-start = (f32[16,8,128]{2,1,0:T(8,128)S(1)}, f32[16,8,128]{2,1,0:T(8,128)}, u32[]{:S(2)}) copy-start(f32[16,8,128]{2,1,0:T(8,128)} %design.3) | copy-start | bytes 196612
  54.2 25.1 %copy-start.1 = (f32[16,8,128]{2,1,0:T(8,128)S(1)}, f32[16,8,128]{2,1,0:T(8,128)}, u32[]{:S(2)}) copy-start(f32[16,8,128]{2,1,0:T(8,128)} %first.1) | copy-start | bytes 196612
  54.2 25.0 %copy-start.2 = (f32[16,8,128]{2,1,0:T(8,128)S(1)}, f32[16,8,128]{2,1,0:T(8,128)}, u32[]{:S(2)}) copy-start(f32[16,8,128]{2,1,0:T(8,128)} %second.1) | copy-start | bytes 196612

commit v4 on v3

--- a/solution.py
+++ b/solution.py
@@ -165,14 +165,23 @@
         pair_rows(corner[2 * m], corner[2 * m + 1], low, turned_x, c1, c2, m)
 
 
-def repack_design_kernel(ra, sb):
+def repack_design_kernel(ra, sb, side, sems):
     b = lax.axis_index("gy")
+    copies = [
+        pltpu.make_async_copy(ra.at[pl.ds(2 * d, 2)], sb.at[d, pl.ds(0, 2)], sems.at[d])
+        for d in range(8)
+    ]
+    for copy in copies:
+        copy.start()
     for dest in range(8):
-        sb[dest, 0] = ra[2 * dest]
-        sb[dest, 1] = ra[2 * dest + 1]
         before = ra[2 * dest - 1] if dest > 0 else jnp.zeros_like(ra[0])
         after = ra[2 * dest + 2] if dest < 7 else jnp.zeros_like(ra[0])
-        sb[dest, 2] = jnp.where(b >= 4, before, after)
+        side[dest] = jnp.where(b >= 4, before, after)
+    last = pltpu.make_async_copy(side, sb.at[:, 2], sems.at[8])
+    last.start()
+    for copy in copies:
+        copy.wait()
+    last.wait()
 
 
 def main_kernel(
@@ -390,11 +399,12 @@
         copy.wait()
 
 
-def adam_kernel(arrived, design, first, second, design_out, first_out, second_out):
+def adam_kernel(arrived, design, first, second, d_hbm, f_hbm, s_hbm, d_new, f_new, s_new, sems):
     b = lax.axis_index("gx") // 2
     _, lane = iotas()
     group = lane // 8
     blocks = [arrived[8 * a + b] for a in range(SHARDS)]
+    copies = []
     for layer in range(DZ):
         total = roll(blocks[0], -8 * layer, 1)
         for a in range(1, SHARDS):
@@ -404,9 +414,18 @@
         second_next = BETA_TWO * second[layer] + (1.0 - BETA_TWO) * gradient * gradient
         update = LEARN_RATE * (first_next / BIAS_ONE)
         update = update / (jnp.sqrt(second_next / BIAS_TWO) + ADAM_FLOOR)
-        design_out[layer] = jnp.clip(design[layer] - update, 0.0, 1.0)
-        first_out[layer] = first_next
-        second_out[layer] = second_next
+        d_new[layer] = jnp.clip(design[layer] - update, 0.0, 1.0)
+        f_new[layer] = first_next
+        s_new[layer] = second_next
+        if layer % 4 == 3:
+            part = pl.ds(layer - 3, 4)
+            outs = ((d_new, d_hbm), (f_new, f_hbm), (s_new, s_hbm))
+            for number, (new, out) in enumerate(outs):
+                slot = sems.at[3 * (layer // 4) + number]
+                copies.append(pltpu.make_async_copy(new.at[part], out.at[part], slot))
+                copies[-1].start()
+    for copy in copies:
+        copy.wait()
 
 
 def f32(*shape):
@@ -503,7 +522,14 @@
     )
     rc1 = swapped(c1, "gx", 0)
     rc2 = swapped(c2, "gx", 1)
-    (sb,) = call(repack_design_kernel, [near_by(8, 3, 2, ROWS, LANES)], (ra,), 4)
+    (sb,) = call(
+        repack_design_kernel,
+        [f32(8, 3, 2, ROWS, LANES)],
+        (ra,),
+        4,
+        [vmem((8, 2, ROWS, LANES), jnp.float32), dma((9,))],
+        far_outs=(0,),
+    )
     rb = lax.all_to_all(sb, "gy", split_axis=0, concat_axis=0, tiled=True)
     extended = vmem((3, NZ, 16, 256), jnp.float32)
     eo, ho, go, ko, send = call(
@@ -536,7 +562,12 @@
     arrived = lax.all_to_all(send, ("gx", "gy"), split_axis=0, concat_axis=0, tiled=True)
     shard = f32(DZ, ROWS, LANES)
     design_next, first_next, second_next = call(
-        adam_kernel, [shard] * 3, (arrived, design, first_moment, second_moment), 4
+        adam_kernel,
+        [shard] * 3,
+        (arrived, design, first_moment, second_moment),
+        4,
+        [vmem((DZ, ROWS, LANES), jnp.float32)] * 3 + [dma((12,))],
+        far_outs=range(3),
     )
     shape = electric.shape
     return (

time: 81.4 us -> 81.5 us (level)
  no operation moved by 1% of the time
where the time goes in v4:
time: 81.5 us; the launch traced here: 81.1 us
  blocking collectives  42.1 us (52%)
  starting transfers between devices  20.5 us (25%)
  Pallas kernels  12.7 us (16%)
  waiting for transfers between devices  4.45 us (5%)
  between operations  1.38 us (2%)
    all_to_all x1, blocking collectives, local(): lax.all_to_all(send, ('gx', 'gy'), split_axis=0, concat_axis=0, tiled=True)  25 us
    all_to_all x1, blocking collectives, local(): ra = lax.all_to_all(sa, 'gx', split_axis=0, concat_axis=0, tiled=True)  17 us
    ppermute x6, starting transfers between devices, swapped(): return lax.ppermute(block, axis, route + [(j, i) for i, j in route])  15.5 us
    pallas_call x5, Pallas kernels, call(): pl.pallas_call(kernel, out_shape=outs, in_specs=[pl.BlockSpec(memory_spac...  12.7 us
    all_to_all x1, starting transfers between devices, local(): rb = lax.all_to_all(sb, 'gy', split_axis=0, concat_axis=0, tiled=True)  5.04 us
    ppermute x6, waiting for transfers between devices, swapped(): return lax.ppermute(block, axis, route + [(j, i) for i, j in route])  4.45 us
  transfers between devices with their start and end apart: 7, of which 2 were waited for; matrix products, arithmetic and copies ran while one was open for 0% of the time, Pallas kernels for 1%

profile of v4, /device:TPU:1, one launch (start us, length us, event | category | flops | bytes accessed | tf_op | source)
XLA Modules:
  0.0 81.1 jit_solution(4893987442529418323)
XLA Ops:
  0.6 2.3 %shard_map.162 = (f32[16,2,8,128]{3,2,1,0:T(8,128)S(1)}, f32[131,8,128]{2,1,0:T(8,128)S(1)}, f32[131,8,128]{2,1,0:T(8,128)S(1)}, f32[17,8,128]{2,1,0:T(8,128)S(1...) custom-call(f32[60,8,128]{2,1,0:T(8,128)} %bitcast.9, f32[60,8,128]{2,1,0:T(8,128)} %bitcast.11, ...), custom_call_target="tpu_custom_call" | custom-call | flops 1000000 | bytes 1000000 | tf_op jit(solution)/shard_map/pallas_call | solution.py:443
  3.0 1.5 %collective-permute-start.2 = (f32[131,8,128]{2,1,0:T(8,128)S(1)}, f32[131,8,128]{2,1,0:T(8,128)S(1)}, u32[]{:S(2)}, u32[]{:S(2)}) collective-permute-start(f32[131,8,128]{2,1,0:T(8,128)S(1)} %get-tuple-element.26), channel_id=1, source_target_pairs={{0,8},{16,24},{32,40},{48,56},{64,72},{80,88},{96,104},{112,120},{... | collective-permute-start | bytes 1609736 | tf_op jit(solution)/shard_map/ppermute | solution.py:467
  4.4 4.8 %collective-permute-start.3 = (f32[131,8,128]{2,1,0:T(8,128)S(1)}, f32[131,8,128]{2,1,0:T(8,128)S(1)}, u32[]{:S(2)}, u32[]{:S(2)}) collective-permute-start(f32[131,8,128]{2,1,0:T(8,128)S(1)} %get-tuple-element.27), channel_id=1, source_target_pairs={{8,16},{24,32},{40,48},{56,64},{72,80},{88,96},{104,112},{16,8},{3... | collective-permute-start | bytes 1609736 | tf_op jit(solution)/shard_map/ppermute | solution.py:467
  9.3 17.0 %all_to_all.15.ra = f32[16,2,8,128]{3,2,1,0:T(8,128)S(1)} all-to-all(f32[16,2,8,128]{3,2,1,0:T(8,128)S(1)} %get-tuple-element.30), channel_id=1, replica_groups=mesh['gx'=16,'gy'=8] {'gx'}, dimensions={0} | all-to-all | bytes 262144 | tf_op jit(solution)/shard_map/all_to_all | solution.py:515
  26.3 0.8 shard_map.164
  27.1 5.0 %all-to-all-start.1 = ((f32[8,3,2,8,128]{4,3,2,1,0:T(8,128)}), f32[8,3,2,8,128]{4,3,2,1,0:T(8,128)S(1)}, u32[]{:S(2)}, u32[]{:S(2)}) async-start(f32[8,3,2,8,128]{4,3,2,1,0:T(8,128)} %shard_map.164), calls=%async_computation.1 | async-start | bytes 393216 | tf_op jit(solution)/shard_map/all_to_all | solution.py:533
  32.1 1.5 %collective-permute-start = (f32[17,8,128]{2,1,0:T(8,128)S(1)}, f32[17,8,128]{2,1,0:T(8,128)S(1)}, u32[]{:S(2)}, u32[]{:S(2)}) collective-permute-start(f32[17,8,128]{2,1,0:T(8,128)S(1)} %get-tuple-element.24), channel_id=1, source_target_pairs={{0,1},{2,3},{4,5},{6,7},{1,0},{3,2},{5,4},{7,6},{8,9},{10,11},{12,... | collective-permute-start | bytes 208904 | tf_op jit(solution)/shard_map/ppermute | solution.py:467
  33.6 0.7 collective-permute-start.1
  34.2 2.3 %collective-permute-done.ry1 = f32[17,8,128]{2,1,0:T(8,128)S(1)} collective-permute-done((f32[17,8,128]{2,1,0:T(8,128)S(1)}, f32[17,8,128]{2,1,0:T(8,128)S(1)}, u32[]{:S(2)}, u32[]{:S(2)}) %collective-permute-start) | collective-permute-done | bytes 69664 | tf_op jit(solution)/shard_map/ppermute | solution.py:467
  36.5 0.0 collective-permute-done.1.ry2
  36.5 0.3 shard_map.163
  36.9 2.8 %collective-permute-start.4 = (f32[17,8,128]{2,1,0:T(8,128)S(1)}, f32[17,8,128]{2,1,0:T(8,128)S(1)}, u32[]{:S(2)}, u32[]{:S(2)}) collective-permute-start(f32[17,8,128]{2,1,0:T(8,128)S(1)} %get-tuple-element.28), channel_id=1, source_target_pairs={{0,8},{16,24},{32,40},{48,56},{64,72},{80,88},{96,104},{112,120},{... | collective-permute-start | bytes 208904 | tf_op jit(solution)/shard_map/ppermute | solution.py:467
  39.6 4.3 %collective-permute-start.5 = (f32[17,8,128]{2,1,0:T(8,128)S(1)}, f32[17,8,128]{2,1,0:T(8,128)S(1)}, u32[]{:S(2)}, u32[]{:S(2)}) collective-permute-start(f32[17,8,128]{2,1,0:T(8,128)S(1)} %get-tuple-element.29), channel_id=1, source_target_pairs={{8,16},{24,32},{40,48},{56,64},{72,80},{88,96},{104,112},{16,8},{3... | collective-permute-start | bytes 208904 | tf_op jit(solution)/shard_map/ppermute | solution.py:467
  44.6 0.0 collective-permute-done.4.rc1
  44.6 2.1 %collective-permute-done.5.rc2 = f32[17,8,128]{2,1,0:T(8,128)S(1)} collective-permute-done((f32[17,8,128]{2,1,0:T(8,128)S(1)}, f32[17,8,128]{2,1,0:T(8,128)S(1)}, u32[]{:S(2)}, u32[]{:S(2)}) %collective-permute-start.5) | collective-permute-done | bytes 69664 | tf_op jit(solution)/shard_map/ppermute | solution.py:467
  46.8 0.0 all-to-all-done.1.rb
  46.8 0.0 collective-permute-done.2.rx1
  46.8 0.0 collective-permute-done.3.rx2
  46.8 7.5 %shard_map.165 = (f32[60,8,128]{2,1,0:T(8,128)}, f32[60,8,128]{2,1,0:T(8,128)}, f32[60,8,128]{2,1,0:T(8,128)}, f32[60,8,128]{2,1,0:T(8,128)}, f32[128,8,128]{2,1,0:T(8,128)S(1)}) custom-call(s32[1]{0:T(128)S(6)} %copy.18.offset_ref, f32[60,8,128]{2,1,0:T(8,128)} %bitcast.10, f32[60,8,128]{2,1,0:T(8,128)} %bitcast.12, f32[60,8,128]{2,1,0:T(8,128)} %bitcast.14, ...), custom_call_target="tpu_custom_call" | custom-call | flops 10000000 | bytes 10000000 | tf_op jit(solution)/shard_map/pallas_call | solution.py:443
  54.3 0.0 copy-start
  54.3 0.0 copy-start.1
  54.3 0.0 copy-start.2
  54.3 25.0 %all_to_all.16.arrived = f32[128,8,128]{2,1,0:T(8,128)S(1)} all-to-all(f32[128,8,128]{2,1,0:T(8,128)S(1)} %get-tuple-element.35), channel_id=1, replica_groups=mesh['gx'=16,'gy'=8] {'gx','gy'}, dimensions={0} | all-to-all | bytes 1048576 | tf_op jit(solution)/shard_map/all_to_all | solution.py:562
  79.3 0.0 copy-done
  79.3 0.0 copy-done.1
  79.3 0.0 copy-done.2
  79.3 1.8 %shard_map.166 = (f32[16,8,128]{2,1,0:T(8,128)}, f32[16,8,128]{2,1,0:T(8,128)}, f32[16,8,128]{2,1,0:T(8,128)}) custom-call(f32[128,8,128]{2,1,0:T(8,128)S(1)} %all_to_all.16.arrived, f32[16,8,128]{2,1,0:T(8,128)S(1)} %copy-done, f32[16,8,128]{2,1,0:T(8,128)S(1)} %copy-done.1, f32[16,8,128]{2,1,0:T(8,128)S(1)} %copy-done.2), custom_call_target="tpu_custom_call" | custom-call | flops 1000000 | bytes 1000000 | tf_op jit(solution)/shard_map/pallas_call | solution.py:443
Async XLA Ops:
  3.0 43.8 %collective-permute-start.2 = (f32[131,8,128]{2,1,0:T(8,128)S(1)}, f32[131,8,128]{2,1,0:T(8,128)S(1)}, u32[]{:S(2)}, u32[]{:S(2)}) collective-permute-start(f32[131,8,128]{2,1,0:T(8,128)S(1)} %get-tuple-element.26), channel_id=1, source_target_pairs={{0,8},{16,24},{32,40},{48,56},{64,72},{80,88},{96,104},{112,120},{... | collective-permute-start | bytes 1609736 | tf_op jit(solution)/shard_map/ppermute | solution.py:467
  4.4 42.3 %collective-permute-start.3 = (f32[131,8,128]{2,1,0:T(8,128)S(1)}, f32[131,8,128]{2,1,0:T(8,128)S(1)}, u32[]{:S(2)}, u32[]{:S(2)}) collective-permute-start(f32[131,8,128]{2,1,0:T(8,128)S(1)} %get-tuple-element.27), channel_id=1, source_target_pairs={{8,16},{24,32},{40,48},{56,64},{72,80},{88,96},{104,112},{16,8},{3... | collective-permute-start | bytes 1609736 | tf_op jit(solution)/shard_map/ppermute | solution.py:467
  27.1 19.7 %all-to-all-start.1 = ((f32[8,3,2,8,128]{4,3,2,1,0:T(8,128)}), f32[8,3,2,8,128]{4,3,2,1,0:T(8,128)S(1)}, u32[]{:S(2)}, u32[]{:S(2)}) async-start(f32[8,3,2,8,128]{4,3,2,1,0:T(8,128)} %shard_map.164), calls=%async_computation.1 | async-start | bytes 393216 | tf_op jit(solution)/shard_map/all_to_all | solution.py:533
  32.1 4.4 %collective-permute-start = (f32[17,8,128]{2,1,0:T(8,128)S(1)}, f32[17,8,128]{2,1,0:T(8,128)S(1)}, u32[]{:S(2)}, u32[]{:S(2)}) collective-permute-start(f32[17,8,128]{2,1,0:T(8,128)S(1)} %get-tuple-element.24), channel_id=1, source_target_pairs={{0,1},{2,3},{4,5},{6,7},{1,0},{3,2},{5,4},{7,6},{8,9},{10,11},{12,... | collective-permute-start | bytes 208904 | tf_op jit(solution)/shard_map/ppermute | solution.py:467
  33.6 3.0 %collective-permute-start.1 = (f32[17,8,128]{2,1,0:T(8,128)S(1)}, f32[17,8,128]{2,1,0:T(8,128)S(1)}, u32[]{:S(2)}, u32[]{:S(2)}) collective-permute-start(f32[17,8,128]{2,1,0:T(8,128)S(1)} %get-tuple-element.25), channel_id=1, source_target_pairs={{1,2},{3,4},{5,6},{2,1},{4,3},{6,5},{9,10},{11,12},{13,14},{10,9},... | collective-permute-start | bytes 208904 | tf_op jit(solution)/shard_map/ppermute | solution.py:467
  36.9 7.7 %collective-permute-start.4 = (f32[17,8,128]{2,1,0:T(8,128)S(1)}, f32[17,8,128]{2,1,0:T(8,128)S(1)}, u32[]{:S(2)}, u32[]{:S(2)}) collective-permute-start(f32[17,8,128]{2,1,0:T(8,128)S(1)} %get-tuple-element.28), channel_id=1, source_target_pairs={{0,8},{16,24},{32,40},{48,56},{64,72},{80,88},{96,104},{112,120},{... | collective-permute-start | bytes 208904 | tf_op jit(solution)/shard_map/ppermute | solution.py:467
  39.6 7.1 %collective-permute-start.5 = (f32[17,8,128]{2,1,0:T(8,128)S(1)}, f32[17,8,128]{2,1,0:T(8,128)S(1)}, u32[]{:S(2)}, u32[]{:S(2)}) collective-permute-start(f32[17,8,128]{2,1,0:T(8,128)S(1)} %get-tuple-element.29), channel_id=1, source_target_pairs={{8,16},{24,32},{40,48},{56,64},{72,80},{88,96},{104,112},{16,8},{3... | collective-permute-start | bytes 208904 | tf_op jit(solution)/shard_map/ppermute | solution.py:467
  54.3 25.1 %copy-start = (f32[16,8,128]{2,1,0:T(8,128)S(1)}, f32[16,8,128]{2,1,0:T(8,128)}, u32[]{:S(2)}) copy-start(f32[16,8,128]{2,1,0:T(8,128)} %design.3) | copy-start | bytes 196612
  54.3 25.1 %copy-start.1 = (f32[16,8,128]{2,1,0:T(8,128)S(1)}, f32[16,8,128]{2,1,0:T(8,128)}, u32[]{:S(2)}) copy-start(f32[16,8,128]{2,1,0:T(8,128)} %first.1) | copy-start | bytes 196612
  54.3 25.0 %copy-start.2 = (f32[16,8,128]{2,1,0:T(8,128)S(1)}, f32[16,8,128]{2,1,0:T(8,128)}, u32[]{:S(2)}) copy-start(f32[16,8,128]{2,1,0:T(8,128)} %second.1) | copy-start | bytes 196612
